TPU v7x, 32 devices: a whole 2x2x4 slice. The times are simulated.
32 devices in a mesh: days: 2 (over x), chan: 4 (over y, core), sect: 4 (over z).
Axes of the slice: x: 2, y: 2, z: 4, core: 2. Of those that a mesh axis runs over, the one named last changes fastest.
Arguments:
- traces: bfloat16 [8, 256, 512], P(('days', 'sect'), 'chan'), parts along dimension 0, may hold values from -6 to 6
- positions: int32 [4, 256], replicated, may hold values from 0 to 255, each once within a row
- partners: int32 [4, 2], replicated, may hold values from 0 to 3, as said below
Outputs:
- stacks: float32 [8, 256, 3, 128], P(('days', 'sect'), 'chan'), parts along dimension 0
There are 2 independent parts, one for each index of `days`. A program takes and returns all parts, laid end to end along the dimension named above; an argument that names none is the same for every part. Nothing has to cross between parts.
Inputs may be any that keep to these rules, and one draw needn't show every extreme that they name: Each row is a permutation of the positions 0 to 255. The sections stand in a circle in some order and r is one round from 1 to 3; partners[s] are the sections r places after and r places before s on that circle (the same section when r = 2), never s itself.
All inputs are finite; a program needn't handle non-finite values.
Results may differ from a plain program's by a relative error of at most 0.0003.
Values may be sent and summed in bfloat16 or wider, within the bound.
No kernel may reach another device: no remote copies, remote signals or barrier semaphores. Data moves between devices by JAX's collectives and lax.ppermute only.
A program may use at most 128 MiB of HBM per device.

v0:
```python
import math

import jax
import jax.numpy as jnp
from jax import lax
from jax.sharding import PartitionSpec as P

LAGS = 64


def windows(block):
    half = LAGS // 2
    width = block.shape[1]
    padded = jnp.pad(block, ((0, 0), (LAGS, LAGS)))
    return jnp.stack(
        [
            padded[:, LAGS + half - lag_index : LAGS + half - lag_index + width]
            for lag_index in range(LAGS)
        ],
        axis=1,
    )


def section_terms(shift_x, places_x, other, places_other):
    count = shift_x.shape[0]
    flat = shift_x.reshape(count * LAGS, shift_x.shape[2])
    correlation = lax.dot_general(
        flat, other, (((1,), (1,)), ((), ())), preferred_element_type=jnp.float32
    )
    correlation = correlation.reshape(count, LAGS, other.shape[0])
    root_mean = jnp.sqrt(jnp.mean(correlation * correlation, axis=1) + 1e-06)
    normed = correlation / root_mean[:, None, :]
    ahead = (places_other[None, :] >= places_x[:, None]).astype(jnp.float32)
    forward = jnp.sum(normed * ahead[:, None, :], axis=2)
    backward = jnp.sum(normed * (1.0 - ahead)[:, None, :], axis=2)
    return jnp.stack([forward, backward], axis=1)


def body(traces, positions, partners):
    rows = traces.shape[1]
    chan_size = lax.axis_size("chan")
    sect_size = lax.axis_size("sect")
    sect_ch = rows * chan_size
    me_sect = lax.axis_index("sect")
    me_chan = lax.axis_index("chan")
    own_places = lax.dynamic_slice(positions, (me_sect, me_chan * rows), (1, rows))[0]
    shift_x = windows(traces[0])
    targets = (me_sect, partners[me_sect, 0], partners[me_sect, 1])
    totals = jnp.zeros((rows, 3, 2, LAGS), jnp.float32)
    whole = lax.all_gather(traces, ("chan", "sect"), axis=1, tiled=True)
    whole = whole.reshape(chan_size, sect_size, rows, whole.shape[2]).transpose(1, 0, 2, 3)
    whole = whole.reshape(sect_size, sect_ch, whole.shape[3])
    zero = jnp.zeros((), jnp.int32)
    for target in range(3):
        section_rows = lax.dynamic_index_in_dim(whole, targets[target], 0, keepdims=False)
        places = lax.dynamic_slice(positions, (targets[target], zero), (1, section_rows.shape[0]))[
            0
        ]
        totals = totals.at[:, target].add(section_terms(shift_x, own_places, section_rows, places))
    scaled = totals * (1.0 / math.sqrt(sect_ch))
    return scaled.reshape(1, rows, 3, 2 * LAGS)


def solution(mesh):
    in_specs = (P(("days", "sect"), "chan", None), P(), P())
    out_specs = P(("days", "sect"), "chan", None, None)
    return jax.shard_map(body, mesh=mesh, in_specs=in_specs, out_specs=out_specs, check_vma=False)
```

profile of v0, /device:TPU:0, one launch (start us, length us, event | category | flops | bytes accessed | tf_op | source)
XLA Modules:
  0.0 97.0 jit_solution(16580105608858722093)
XLA Ops:
  7.3 1.4 %constant_dynamic-slice_fusion.4 = (s32[1,1]{0,1:T(1,128)}, s32[1,1]{0,1:T(1,128)}) fusion(s32[4,2]{0,1:T(2,128)} %param.11, s32[]{:T(128)S(6)} %select_n.19), kind=kLoop, calls=%fused_computation.107 | loop fusion | bytes 20 | tf_op jit(solution)/shard_map/dynamic_slice | solution.py:48
  11.4 1.6 %slice_bitcast_fusion.6 = (bf16[64,1,512]{2,0,1:T(8,128)(2,1)S(1)}, bf16[64,1,512]{2,0,1:T(8,128)(2,1)S(1)}, bf16[64,1,512]{2,0,1:T(8,128)(2,1)S(1)}, bf16[64,1,...) fusion(bf16[64,512]{1,0:T(8,128)(2,1)} %bitcast.178), kind=kLoop, calls=%fused_computation.37 | loop fusion | bytes 655360 | tf_op jit(solution)/shard_map/stack | solution.py:15
  13.1 1.6 %slice_bitcast_fusion = (bf16[64,1,512]{2,0,1:T(8,128)(2,1)S(1)}, bf16[64,1,512]{2,0,1:T(8,128)(2,1)S(1)}, bf16[64,1,512]{2,0,1:T(8,128)(2,1)S(1)}, bf16[64,1,51...) fusion(bf16[64,512]{1,0:T(8,128)(2,1)} %bitcast.179), kind=kLoop, calls=%fused_computation.31 | loop fusion | bytes 655360 | tf_op jit(solution)/shard_map/stack | solution.py:15
  15.6 1.6 %slice_bitcast_fusion.1 = (bf16[64,1,512]{2,0,1:T(8,128)(2,1)S(1)}, bf16[64,1,512]{2,0,1:T(8,128)(2,1)S(1)}, bf16[64,1,512]{2,0,1:T(8,128)(2,1)S(1)}, bf16[64,1,...) fusion(bf16[64,512]{1,0:T(8,128)(2,1)} %bitcast.180), kind=kLoop, calls=%fused_computation.32 | loop fusion | bytes 655360 | tf_op jit(solution)/shard_map/stack | solution.py:15
  20.3 0.8 copy.2014
  21.1 0.8 copy.2015
  22.6 0.8 copy.2017
  23.4 0.8 copy.2018
  24.1 0.8 copy.2019
  31.1 0.8 copy.2028
  37.3 0.8 copy.2036
  38.1 0.8 copy.2037
  41.1 0.8 copy.2041
  41.8 0.8 copy.2042
  42.6 0.8 copy.2043
  43.3 0.8 copy.2044
  49.9 27.4 %stack.286 = bf16[64,64,512]{2,1,0:T(8,128)(2,1)} concatenate(bf16[64,1,512]{2,1,0:T(2,128)(2,1)S(1)} %copy.1987, bf16[64,1,512]{2,1,0:T(2,128)(2,1)S(1)} %copy.1988, bf16[64,1,512]{2,1,0:T(2,128)(2,1)S(1)} %copy.1989, bf16[64,1,512]{2,1,0:T(2,128)(2,1)S(1)} %copy.1990, bf16[64,1,512]{2,1,0:T(2,128)(2,1)S(1)} %copy.1991, bf16[64,1,512]{2,1,0:T(2,128)(2,1)S(1)} %copy.1992, ...), dimensions={1} | concatenate | bytes 8388608 | tf_op jit(solution)/shard_map/stack | solution.py:15
  77.6 1.3 %copy.2051 = bf16[4,4,64,512]{3,2,1,0:T(8,128)(2,1)S(1)} copy(bf16[4,4,64,512]{3,2,0,1:T(8,128)(2,1)} %bitcast.189) | data formatting | bytes 2097152 | tf_op jit(solution)/shard_map/transpose | solution.py:51
  79.0 3.6 %multiply_reduce_fusion.8 = (f32[64,256]{1,0:T(8,128)S(1)}, f32[64,64,256]{2,1,0:T(8,128)S(1)}) fusion(bf16[64,64,512]{2,1,0:T(8,128)(2,1)} %stack.286, bf16[4,256,512]{2,1,0:T(8,128)(2,1)S(1)} %bitcast.186, s32[]{:T(128)S(6)} %select_n.19), kind=kOutput, calls=%fused_computation.8 | convolution fusion | flops 1075822592 | bytes 8716292 | tf_op jit(solution)/shard_map/dot_general | solution.py:27
  82.6 1.3 %multiply_reduce_fusion.2 = (f32[64,256]{1,0:T(8,128)S(1)}, f32[64,64,256]{2,1,0:T(8,128)S(1)}) fusion(bf16[64,64,512]{2,1,0:T(8,128)(2,1)S(1)} %copy-done, bf16[4,256,512]{2,1,0:T(8,128)(2,1)S(1)} %bitcast.187, s32[]{:T(128)S(6)} %select_n.22), kind=kOutput, calls=%fused_computation.2 | convolution fusion | flops 1075822592 | bytes 8716292 | tf_op jit(solution)/shard_map/dot_general | solution.py:27
  83.9 1.3 %multiply_reduce_fusion.5 = (f32[64,256]{1,0:T(8,128)S(1)}, f32[64,64,256]{2,1,0:T(8,128)S(1)}) fusion(bf16[64,64,512]{2,1,0:T(8,128)(2,1)S(1)} %copy-done, bf16[4,256,512]{2,1,0:T(8,128)(2,1)S(1)} %bitcast.188, s32[]{:T(128)S(6)} %select_n.21), kind=kOutput, calls=%fused_computation.5 | convolution fusion | flops 1075822592 | bytes 8716292 | tf_op jit(solution)/shard_map/dot_general | solution.py:27
  85.3 1.2 %multiply_reduce_fusion.7 = (f32[64,64]{1,0:T(8,128)S(1)}, f32[64,64]{1,0:T(8,128)S(1)}) fusion(f32[64,256]{1,0:T(8,128)S(1)} %get-tuple-element.120, f32[64,64,256]{2,1,0:T(8,128)S(1)} %get-tuple-element.122, f32[64,256]{1,0:T(8,128)S(1)} %add_sqrt_fusion.2, f32[64,256]{1,0:T(8,128)S(1)} %get-tuple-element.117), kind=kLoop, calls=%fused_computation.7 | loop fusion | flops 5234688 | bytes 4423680 | tf_op jit(solution)/shard_map/reduce_sum | solution.py:34
  86.6 2.4 %multiply_reduce_fusion.1 = (f32[64,64]{1,0:T(8,128)S(1)}, f32[64,64]{1,0:T(8,128)S(1)}, f32[64,64]{1,0:T(8,128)S(1)}, f32[64,64]{1,0:T(8,128)S(1)}) fusion(f32[64,256]{1,0:T(8,128)S(1)} %get-tuple-element.118, f32[64,64,256]{2,1,0:T(8,128)S(1)} %get-tuple-element.126, f32[64,256]{1,0:T(8,128)S(1)} %add_sqrt_fusion, f32[64,256]{1,0:T(8,128)S(1)} %get-tuple-element.115, ...), kind=kLoop, calls=%fused_computation.1 | loop fusion | flops 10469376 | bytes 8847360 | tf_op jit(solution)/shard_map/reduce_sum | solution.py:34
  89.3 0.8 reshape.306
  (77 shorter events, 24.5 us)
Async XLA Ops:
  6.5 11.5 %copy-start.1 = (bf16[1,64,512]{2,1,0:T(8,128)(2,1)S(1)}, bf16[1,64,512]{2,1,0:T(8,128)(2,1)}, u32[]{:S(2)}) copy-start(bf16[1,64,512]{2,1,0:T(8,128)(2,1)} %param.9) | copy-start | bytes 196612
  6.5 71.1 %all-gather.2.cloned.1.call-start = ((), (), s32[]{:S(2)}) async-start(), calls=%async_computation | async-start | bytes 1114112 | tf_op jit(solution)/shard_map/all_gather | solution.py:50
  49.9 27.4 %copy-start.2 = (s32[4,256]{1,0:T(4,128)S(1)}, s32[4,256]{1,0:T(4,128)}, u32[]{:S(2)}) copy-start(s32[4,256]{1,0:T(4,128)} %param.10) | copy-start | bytes 12292
  78.9 3.7 %copy-start = (bf16[64,64,512]{2,1,0:T(8,128)(2,1)S(1)}, bf16[64,64,512]{2,1,0:T(8,128)(2,1)}, u32[]{:S(2)}) copy-start(bf16[64,64,512]{2,1,0:T(8,128)(2,1)} %stack.286) | copy-start | bytes 12582916
Sparse Core Ops, SparseCore 0:
  9.6 40.6 all-gather.1
where the time goes:
time: 98.7 us; the launch traced here: 97 us
  local copies, waits for them, and re-layouts  68 us (69%)
  between operations  17.8 us (18%)
  matrix products  6.24 us (6%)
  other arithmetic  4.14 us (4%)
    another operation x72, local copies, waits for them, and re-layouts, windows(): jnp.stack([padded[:, LAGS + half - lag_index:LAGS + half - lag_index + wi...  64.3 us
    dot_general x3, matrix products, section_terms(): lax.dot_general(flat, other, (((1,), (1,)), ((), ())), preferred_element_...  6.24 us
    reduce_sum x2, other arithmetic, section_terms(): forward = jnp.sum(normed * ahead[:, None, :], axis=2)  3.53 us
  transfers between devices with their start and end apart: 1, of which 0 were waited for; matrix products, arithmetic and copies ran while one was open for 68% of the time, Pallas kernels for 0%

commit v1 on v0

v1 whole, which is shorter than its diff:
```python
import functools
import math

import jax
import jax.numpy as jnp
from jax import lax
from jax.experimental import pallas as pl
from jax.experimental.pallas import tpu as pltpu
from jax.sharding import PartitionSpec as P

LAGS = 64
HALF = LAGS // 2
LANES = 128
TILE = 256


def build_windows(x, t_ref):
    rows, width = x.shape
    lane = lax.broadcasted_iota(jnp.int32, (rows, width), 1)
    zero = jnp.zeros_like(x)
    for lag in range(LAGS):
        shift = HALF - lag
        start = (2 * (lag % HALF) + lag // HALF) * rows
        moved = x
        if shift != 0:
            inside = (lane < width - shift) if shift > 0 else (lane >= -shift)
            moved = jnp.where(inside, pltpu.roll(x, (-shift) % width, 1), zero)
        t_ref[pl.ds(start, rows), :] = moved


def stack_kernel(
    sel_ref, x_ref, g_ref, pos_ref, own_ref, o_ref, t_ref, c_ref, w_ref, acc_ref, *, blk, nblk, scale
):
    rows = x_ref.shape[0]
    build_windows(x_ref[...], t_ref)
    ncol = LAGS * rows // LANES
    own = own_ref[...]
    for k in range(3):
        q = sel_ref[k]
        acc_ref[...] = jnp.zeros_like(acc_ref)

        @pl.loop(0, nblk)
        def _(b):
            xq = g_ref[q, pl.ds(b * blk, blk), :]
            power = jnp.zeros((blk, LANES), jnp.float32)
            for n in range(LAGS * rows // TILE):
                cols = slice(n * TILE, (n + 1) * TILE)
                c = lax.dot_general(
                    xq,
                    t_ref[cols, :],
                    (((1,), (1,)), ((), ())),
                    preferred_element_type=jnp.float32,
                )
                c_ref[:, cols] = c
                for h in range(TILE // LANES):
                    part = c[:, h * LANES : (h + 1) * LANES]
                    power = power + part * part
            power = power + pltpu.roll(power, rows, 1)
            w = scale / jnp.sqrt(power * (1.0 / LAGS) + 1e-6)
            row = pos_ref[q, :, pl.ds(b * blk, blk)]
            column = jnp.transpose(jnp.broadcast_to(row, (8, blk)))[:, 0:1]
            ahead = column >= own
            w_ref[0] = jnp.where(ahead, w, 0.0)
            w_ref[1] = jnp.where(ahead, 0.0, w)
            for n in range(ncol):
                part = c_ref[:, n * LANES : (n + 1) * LANES]
                for side in range(2):
                    total = jnp.sum(part * w_ref[side], axis=0, keepdims=True)
                    acc_ref[pl.ds(side * ncol + n, 1), :] += total

        turned = jnp.transpose(acc_ref[...])
        o_ref[:, k, :] = jnp.concatenate(
            [turned[p * rows : (p + 1) * rows, s * ncol : (s + 1) * ncol] for s in range(2) for p in range(2)],
            axis=1,
        )


def stacks_of(sel, x, g, places, own):
    rows, width = x.shape
    sections, count, _ = g.shape
    ncol = LAGS * rows // LANES
    vmem = pl.BlockSpec(memory_space=pltpu.VMEM)
    return pl.pallas_call(
        functools.partial(stack_kernel, blk=TILE, nblk=count // TILE, scale=1.0 / math.sqrt(count)),
        out_shape=jax.ShapeDtypeStruct((rows, 3, 2 * LAGS), jnp.float32),
        in_specs=[pl.BlockSpec(memory_space=pltpu.SMEM)] + [vmem] * 4,
        out_specs=vmem,
        scratch_shapes=[
            pltpu.VMEM((LAGS * rows, width), jnp.bfloat16),
            pltpu.VMEM((TILE, LAGS * rows), jnp.float32),
            pltpu.VMEM((2, TILE, LANES), jnp.float32),
            pltpu.VMEM((2 * ncol, LANES), jnp.float32),
        ],
        compiler_params=pltpu.CompilerParams(vmem_limit_bytes=48 << 20),
    )(sel, x, g, places, own)


def flip(x, axis, bit):
    n = lax.axis_size(axis)
    return lax.ppermute(x, axis, [(d, d ^ bit) for d in range(n)])


def body(traces, positions, partners):
    x = traces[0]
    rows = x.shape[0]
    chans = lax.axis_size("chan")
    sections = lax.axis_size("sect")
    me = lax.axis_index("sect")
    chan = lax.axis_index("chan")
    targets = jnp.stack([me, partners[me, 0], partners[me, 1]])
    places = positions.astype(jnp.float32).reshape(sections, chans, rows)
    own = places[me, chan]
    own = jnp.concatenate([own, own])[None]
    if chans == 4 and sections == 4:
        pieces = [x] + [flip(x, "sect", k) for k in (1, 2, 3)]
        held = jnp.stack(pieces)[targets ^ me]
        held = jnp.stack([held, flip(held, "chan", 2)], axis=1)
        held = jnp.concatenate([held, flip(held, "chan", 1)], axis=1)
        order = chan ^ jnp.array([0, 2, 1, 3], jnp.int32)
        places = places[targets][:, order]
        whole = held.reshape(3, chans * rows, x.shape[1])
        sel = jnp.arange(3, dtype=jnp.int32)
    else:
        whole = lax.all_gather(x, "chan", axis=0, tiled=True)
        whole = lax.all_gather(whole[None], "sect", axis=0, tiled=True)
        sel = targets
    places = places.reshape(places.shape[0], 1, chans * rows)
    return stacks_of(sel, x, whole, places, own)[None]


def solution(mesh):
    in_specs = (P(("days", "sect"), "chan", None), P(), P())
    out_specs = P(("days", "sect"), "chan", None, None)
    return jax.shard_map(body, mesh=mesh, in_specs=in_specs, out_specs=out_specs, check_vma=False)
```

time: 98.7 us -> 28.5 us (0.29); the launches traced: 97 us -> 28.3 us
  local copies, waits for them, and re-layouts: 68 us -> 4.01 us
  between operations: 17.8 us -> 0.09 us
  Pallas kernels: 0 us -> 7.4 us
  starting transfers between devices: 0.01 us -> 7.27 us
  waiting for transfers between devices: 0.73 us -> 7.22 us
  matrix products: 6.24 us -> 0 us
  other arithmetic: 4.14 us -> 2.33 us
    another operation x72 -> x0, local copies, waits for them, and re-layouts: 64.3 us -> none  [windows(): jnp.stack([padded[:, LAGS + half - lag_index:LAGS + half - lag_index + wi...]
    pallas_call x0 -> x1, Pallas kernels: none -> 7.4 us  [stacks_of(): pl.pallas_call(functools.partial(stack_kernel, blk=TILE, nblk=count // TI...]
    ppermute x0 -> x5, starting transfers between devices: none -> 7.27 us  [flip(): return lax.ppermute(x, axis, [(d, d ^ bit) for d in range(n)])]
    ppermute x0 -> x5, waiting for transfers between devices: none -> 7.22 us  [flip(): return lax.ppermute(x, axis, [(d, d ^ bit) for d in range(n)])]
    dot_general x3 -> x0, matrix products: 6.24 us -> none  [section_terms(): lax.dot_general(flat, other, (((1,), (1,)), ((), ())), preferred_element_...]
    reduce_sum x2 -> x0, other arithmetic: 3.53 us -> none  [section_terms(): forward = jnp.sum(normed * ahead[:, None, :], axis=2)]
    gather x0 -> x5, local copies, waits for them, and re-layouts: none -> 1.71 us  [the longest x4 1.15 us: body(): places = places[targets][:, order]]
    select_n x0 -> x3, other arithmetic: none -> 1.39 us  [the longest x2 1.38 us: body(): places = places[targets][:, order]]
  transfers between devices with their start and end apart: 1 -> 5, of which waited for: 0 -> 4; matrix products, arithmetic and copies ran while one was open for 68% -> 17% of each run, Pallas kernels for 0% -> 0%
where the time goes in v1:
time: 28.5 us; the launch traced here: 28.3 us
  Pallas kernels  7.4 us (26%)
  starting transfers between devices  7.27 us (26%)
  waiting for transfers between devices  7.22 us (25%)
  local copies, waits for them, and re-layouts  4.01 us (14%)
  other arithmetic  2.33 us (8%)
    pallas_call x1, Pallas kernels, stacks_of(): pl.pallas_call(functools.partial(stack_kernel, blk=TILE, nblk=count // TI...  7.4 us
    ppermute x5, starting transfers between devices, flip(): return lax.ppermute(x, axis, [(d, d ^ bit) for d in range(n)])  7.27 us
    ppermute x5, waiting for transfers between devices, flip(): return lax.ppermute(x, axis, [(d, d ^ bit) for d in range(n)])  7.22 us
    dynamic_slice x1, local copies, waits for them, and re-layouts, body(): targets = jnp.stack([me, partners[me, 0], partners[me, 1]])  1.41 us
    select_n x2, other arithmetic, body(): places = places[targets][:, order]  1.38 us
    gather x4, local copies, waits for them, and re-layouts, body(): places = places[targets][:, order]  1.15 us
    convert_element_type x1, other arithmetic, body(): places = positions.astype(jnp.float32).reshape(sections, chans, rows)  0.69 us
    broadcast_in_dim x1, local copies, waits for them, and re-layouts, body(): return stacks_of(sel, x, whole, places, own)[None]  0.65 us
  transfers between devices with their start and end apart: 5, of which 4 were waited for; matrix products, arithmetic and copies ran while one was open for 17% of the time, Pallas kernels for 0%

profile of v1, /device:TPU:0, one launch (start us, length us, event | category | flops | bytes accessed | tf_op | source)
XLA Modules:
  0.0 28.3 jit_solution(9963835841075397404)
XLA Ops:
  0.0 3.0 %collective-permute-start = (bf16[64,512]{1,0:T(8,128)(2,1)}, bf16[64,512]{1,0:T(8,128)(2,1)S(1)}, u32[]{:S(2)}, u32[]{:S(2)}) collective-permute-start(bf16[64,512]{1,0:T(8,128)(2,1)} %bitcast.20), channel_id=1, source_target_pairs={{0,1},{1,0},{2,3},{3,2},{4,5},{5,4},{6,7},{7,6},{8,9},{9,8},{10,11... | collective-permute-start | bytes 196616 | tf_op jit(solution)/shard_map/ppermute | solution.py:100
  3.0 2.6 %collective-permute-start.1 = (bf16[64,512]{1,0:T(8,128)(2,1)}, bf16[64,512]{1,0:T(8,128)(2,1)S(1)}, u32[]{:S(2)}, u32[]{:S(2)}) collective-permute-start(bf16[64,512]{1,0:T(8,128)(2,1)} %bitcast.21), channel_id=1, source_target_pairs={{0,2},{1,3},{2,0},{3,1},{4,6},{5,7},{6,4},{7,5},{8,10},{9,11},{10,... | collective-permute-start | bytes 196616 | tf_op jit(solution)/shard_map/ppermute | solution.py:100
  5.6 0.0 collective-permute-start.2
  5.6 1.4 %constant_dynamic-slice_fusion.1 = (s32[1,1]{0,1:T(1,128)}, s32[1,1]{0,1:T(1,128)}) fusion(s32[4,2]{0,1:T(2,128)} %param.6, s32[]{:T(128)S(6)} %select_n.31), kind=kLoop, calls=%fused_computation.18 | loop fusion | bytes 20 | tf_op jit(solution)/shard_map/dynamic_slice | solution.py:110
  7.0 1.4 %fusion.1 = (s32[3]{0:T(128)S(1)}, s32[3,1]{0,1:T(1,128)S(1)}) fusion(s32[1,1]{0,1:T(1,128)} %get-tuple-element.8, s32[1,1]{0,1:T(1,128)} %get-tuple-element.7, s32[1,1]{0,1:T(1,128)} %bitcast.4), kind=kLoop, calls=%fused_computation.13 | loop fusion | flops 15 | bytes 36 | tf_op jit(solution)/shard_map/select_n | solution.py:120
  8.4 0.7 %convert_element_type.3 = f32[4,256]{1,0:T(4,128)S(1)} convert(s32[4,256]{1,0:T(4,128)} %param.5) | non-fusion elementwise | flops 1024 | bytes 8192 | tf_op jit(solution)/shard_map/convert_element_type | solution.py:111
  9.1 0.1 reshape.163
  9.2 0.0 collective-permute-done
  9.2 1.3 %collective-permute-done.1 = bf16[64,512]{1,0:T(8,128)(2,1)S(1)} collective-permute-done((bf16[64,512]{1,0:T(8,128)(2,1)}, bf16[64,512]{1,0:T(8,128)(2,1)S(1)}, u32[]{:S(2)}, u32[]{:S(2)}) %collective-permute-start.1) | collective-permute-done | bytes 65568 | tf_op jit(solution)/shard_map/ppermute | solution.py:100
  10.5 1.4 %collective-permute-done.2 = bf16[64,512]{1,0:T(8,128)(2,1)S(1)} collective-permute-done((bf16[64,512]{1,0:T(8,128)(2,1)}, bf16[64,512]{1,0:T(8,128)(2,1)S(1)}, u32[]{:S(2)}, u32[]{:S(2)}) %collective-permute-start.2) | collective-permute-done | bytes 65568 | tf_op jit(solution)/shard_map/ppermute | solution.py:100
  12.0 0.0 copy-start.1
  12.0 0.6 %gather_fusion = bf16[3,64,512]{2,1,0:T(8,128)(2,1)S(1)} fusion(bf16[4,64,512]{2,1,0:T(8,128)(2,1)S(1)} %pad_maximum_fusion.2, s32[1024]{0:T(1024)S(1)} %pad_clamp_fusion.2), kind=kCustom, calls=%fused_computation | custom fusion | bytes 393228 | tf_op jit(solution)/shard_map/gather | solution.py:116
  12.5 1.6 %collective-permute-start.3 = (bf16[3,64,512]{2,1,0:T(8,128)(2,1)S(1)}, bf16[3,64,512]{2,1,0:T(8,128)(2,1)S(1)}, u32[]{:S(2)}, u32[]{:S(2)}) collective-permute-start(bf16[3,64,512]{2,1,0:T(8,128)(2,1)S(1)} %gather_fusion), channel_id=1, source_target_pairs={{0,8},{4,12},{8,0},{12,4},{1,9},{5,13},{9,1},{13,5},{2,10},{6,14},... | collective-permute-start | bytes 589832 | tf_op jit(solution)/shard_map/ppermute | solution.py:100
  14.1 4.1 %collective-permute-done.3 = bf16[3,64,512]{2,1,0:T(8,128)(2,1)S(1)} collective-permute-done((bf16[3,64,512]{2,1,0:T(8,128)(2,1)S(1)}, bf16[3,64,512]{2,1,0:T(8,128)(2,1)S(1)}, u32[]{:S(2)}, u32[]{:S(2)}) %collective-permute-start.3) | collective-permute-done | bytes 196640 | tf_op jit(solution)/shard_map/ppermute | solution.py:100
  18.3 0.1 collective-permute-start.4
  18.4 0.6 %gather_fusion.1 = f32[3,4,64]{2,1,0:T(4,128)S(1)} fusion(f32[4,4,64]{2,1,0:T(4,128)S(1)} %reshape.163, s32[1024]{0:T(1024)S(1)} %pad_clamp_fusion.1), kind=kCustom, calls=%fused_computation.1 | custom fusion | bytes 6156 | tf_op jit(solution)/shard_map/gather | solution.py:120
  19.0 0.6 %gather_fusion.2 = f32[4,3,64]{2,1,0:T(4,128)S(1)} fusion(f32[3,4,64]{2,0,1:T(4,128)S(1)} %copy.11, s32[1024]{0:T(1024)S(1)} %pad_clamp_fusion), kind=kCustom, calls=%fused_computation.2 | custom fusion | bytes 6160 | tf_op jit(solution)/shard_map/gather | solution.py:120
  19.6 0.1 reshape.164.pos_ref
  19.7 0.1 maximum_bitcast_fusion.own_ref
  19.8 0.4 %collective-permute-done.4 = bf16[3,2,64,512]{3,2,0,1:T(8,128)(2,1)S(1)} collective-permute-done((bf16[3,2,64,512]{3,2,0,1:T(8,128)(2,1)S(1)}, bf16[3,2,64,512]{3,2,0,1:T(8,128)(2,1)S(1)}, u32[]{:S(2)}, u32[]{:S(2)}) %collective-permute-start.4) | collective-permute-done | bytes 393248 | tf_op jit(solution)/shard_map/ppermute | solution.py:100
  20.1 0.1 pad_maximum_fusion
  20.2 0.1 copy.10
  20.3 7.4 %shard_map.46 = f32[64,3,128]{2,1,0:T(4,128)S(1)} custom-call(s32[3]{0:T(128)S(1)} %iota.3.sel_ref, bf16[64,512]{1,0:T(8,128)(2,1)S(1)} %bitcast.23, bf16[3,256,512]{2,1,0:T(8,128)(2,1)S(1)} %bitcast.18, f32[3,1,256]{2,1,0:T(1,128)S(1)} %reshape.164.pos_ref, f32[1,128]{1,0:T(1,128)S(1)} %maximum_bitcast_fusion.own_ref), custom_call_target="tpu_custom_call" | custom-call | tf_op jit(solution)/shard_map/pallas_call | solution.py:83
  27.7 0.6 %copy.13 = f32[1,64,3,128]{3,1,2,0:T(8,128)} copy(f32[1,64,3,128]{3,2,1,0:T(4,128)S(1)} %bitcast.19) | data formatting | bytes 196608 | tf_op jit(solution)/shard_map/broadcast_in_dim | solution.py:128
  (14 shorter events, 0.1 us)
Async XLA Ops:
  0.0 11.9 %copy-start = (bf16[1,64,512]{2,1,0:T(8,128)(2,1)S(1)}, bf16[1,64,512]{2,1,0:T(8,128)(2,1)}, u32[]{:S(2)}) copy-start(bf16[1,64,512]{2,1,0:T(8,128)(2,1)} %param.4) | copy-start | bytes 196612
  0.0 9.2 %collective-permute-start = (bf16[64,512]{1,0:T(8,128)(2,1)}, bf16[64,512]{1,0:T(8,128)(2,1)S(1)}, u32[]{:S(2)}, u32[]{:S(2)}) collective-permute-start(bf16[64,512]{1,0:T(8,128)(2,1)} %bitcast.20), channel_id=1, source_target_pairs={{0,1},{1,0},{2,3},{3,2},{4,5},{5,4},{6,7},{7,6},{8,9},{9,8},{10,11... | collective-permute-start | bytes 196616 | tf_op jit(solution)/shard_map/ppermute | solution.py:100
  3.0 7.5 %collective-permute-start.1 = (bf16[64,512]{1,0:T(8,128)(2,1)}, bf16[64,512]{1,0:T(8,128)(2,1)S(1)}, u32[]{:S(2)}, u32[]{:S(2)}) collective-permute-start(bf16[64,512]{1,0:T(8,128)(2,1)} %bitcast.21), channel_id=1, source_target_pairs={{0,2},{1,3},{2,0},{3,1},{4,6},{5,7},{6,4},{7,5},{8,10},{9,11},{10,... | collective-permute-start | bytes 196616 | tf_op jit(solution)/shard_map/ppermute | solution.py:100
  5.6 6.3 %collective-permute-start.2 = (bf16[64,512]{1,0:T(8,128)(2,1)}, bf16[64,512]{1,0:T(8,128)(2,1)S(1)}, u32[]{:S(2)}, u32[]{:S(2)}) collective-permute-start(bf16[64,512]{1,0:T(8,128)(2,1)} %bitcast.22), channel_id=1, source_target_pairs={{0,3},{1,2},{2,1},{3,0},{4,7},{5,6},{6,5},{7,4},{8,11},{9,10},{10,... | collective-permute-start | bytes 196616 | tf_op jit(solution)/shard_map/ppermute | solution.py:100
  12.0 2.2 %copy-start.1 = (s32[4]{0:T(128)S(1)}, s32[4]{0:T(128)}, u32[]{:S(2)}) copy-start(s32[4]{0:T(128)} %constant.5.clone) | copy-start | bytes 52
  12.5 5.7 %collective-permute-start.3 = (bf16[3,64,512]{2,1,0:T(8,128)(2,1)S(1)}, bf16[3,64,512]{2,1,0:T(8,128)(2,1)S(1)}, u32[]{:S(2)}, u32[]{:S(2)}) collective-permute-start(bf16[3,64,512]{2,1,0:T(8,128)(2,1)S(1)} %gather_fusion), channel_id=1, source_target_pairs={{0,8},{4,12},{8,0},{12,4},{1,9},{5,13},{9,1},{13,5},{2,10},{6,14},... | collective-permute-start | bytes 589832 | tf_op jit(solution)/shard_map/ppermute | solution.py:100
  18.3 1.8 %collective-permute-start.4 = (bf16[3,2,64,512]{3,2,0,1:T(8,128)(2,1)S(1)}, bf16[3,2,64,512]{3,2,0,1:T(8,128)(2,1)S(1)}, u32[]{:S(2)}, u32[]{:S(2)}) collective-permute-start(bf16[3,2,64,512]{3,2,0,1:T(8,128)(2,1)S(1)} %pad_maximum_fusion.1), channel_id=1, source_target_pairs={{0,4},{4,0},{8,12},{12,8},{1,5},{5,1},{9,13},{13,9},{2,6},{6,2},{1... | collective-permute-start | bytes 1179656 | tf_op jit(solution)/shard_map/ppermute | solution.py:100

commit v2 on v0

v2 whole, which is shorter than its diff:
```python
import functools
import math

import jax
import jax.numpy as jnp
from jax import lax
from jax.experimental import pallas as pl
from jax.experimental.pallas import tpu as pltpu
from jax.sharding import PartitionSpec as P

LAGS = 64
HALF = LAGS // 2
LANES = 128
TILE = 256
VMEM = pl.BlockSpec(memory_space=pltpu.VMEM)
SMEM = pl.BlockSpec(memory_space=pltpu.SMEM)


def build_windows(x, t_ref):
    rows, width = x.shape
    lane = lax.broadcasted_iota(jnp.int32, (rows, width), 1)
    zero = jnp.zeros_like(x)
    for lag in range(LAGS):
        shift = HALF - lag
        start = (2 * (lag % HALF) + lag // HALF) * rows
        moved = x
        if shift != 0:
            inside = (lane < width - shift) if shift > 0 else (lane >= -shift)
            moved = jnp.where(inside, pltpu.roll(x, (-shift) % width, 1), zero)
        t_ref[pl.ds(start, rows), :] = moved


def products(xq, t_ref, c_ref):
    power = jnp.zeros((xq.shape[0], LANES), jnp.float32)
    for n in range(t_ref.shape[0] // TILE):
        cols = slice(n * TILE, (n + 1) * TILE)
        c = lax.dot_general(
            xq, t_ref[cols, :], (((1,), (1,)), ((), ())), preferred_element_type=jnp.float32
        )
        c_ref[:, cols] = c
        for h in range(TILE // LANES):
            part = c[:, h * LANES : (h + 1) * LANES]
            power = power + part * part
    return power + pltpu.roll(power, LANES // 2, 1)


def column_of(row):
    return jnp.transpose(jnp.broadcast_to(row, (8, row.shape[1])))[:, 0:1]


def weigh(power, columns, own, w_ref, scale):
    w = scale / jnp.sqrt(power * (1.0 / LAGS) + 1e-6)
    ahead = columns >= own
    w_ref[0] = jnp.where(ahead, w, 0.0)
    w_ref[1] = jnp.where(ahead, 0.0, w)


def side_sums(c_ref, w_ref, low, high, put):
    ncol = c_ref.shape[1] // LANES
    for n in range(ncol):
        part = c_ref[low:high, n * LANES : (n + 1) * LANES]
        for side in range(2):
            put(side * ncol + n, jnp.sum(part * w_ref[side, low:high], axis=0, keepdims=True))


def by_channel(sums, rows):
    ncol = sums.shape[0] // 2
    turned = jnp.transpose(sums)
    return jnp.concatenate(
        [
            turned[p * rows : (p + 1) * rows, s * ncol : (s + 1) * ncol]
            for s in range(2)
            for p in range(2)
        ],
        axis=1,
    )


def stack_kernel(
    sel_ref, x_ref, g_ref, pos_ref, own_ref, o_ref, t_ref, c_ref, w_ref, acc_ref, *, nblk, scale
):
    rows = x_ref.shape[0]
    build_windows(x_ref[...], t_ref)
    own = own_ref[...]
    for k in range(3):
        q = sel_ref[k]
        acc_ref[...] = jnp.zeros_like(acc_ref)

        @pl.loop(0, nblk)
        def _(b):
            power = products(g_ref[q, pl.ds(b * TILE, TILE), :], t_ref, c_ref)
            columns = column_of(pos_ref[q, :, pl.ds(b * TILE, TILE)])
            weigh(power, columns, own, w_ref, scale)

            def put(row, value):
                acc_ref[pl.ds(row, 1), :] += value

            side_sums(c_ref, w_ref, 0, TILE, put)

        o_ref[:, k, :] = by_channel(acc_ref[...], rows)


def scratch(rows, width):
    return [
        pltpu.VMEM((LAGS * rows, width), jnp.bfloat16),
        pltpu.VMEM((TILE, LAGS * rows), jnp.float32),
        pltpu.VMEM((2, TILE, LANES), jnp.float32),
    ]


def sums_shape(rows, count=None):
    shape = (2 * LAGS * rows // LANES, LANES)
    return shape if count is None else (count,) + shape


PARAMS = pltpu.CompilerParams(vmem_limit_bytes=48 << 20)


def stacks_anywhere(x, traces, positions, targets, me, chan):
    rows, width = x.shape
    chans, sections = lax.axis_size("chan"), lax.axis_size("sect")
    count = chans * rows
    whole = lax.all_gather(x, "chan", axis=0, tiled=True)
    whole = lax.all_gather(whole[None], "sect", axis=0, tiled=True)
    places = positions.astype(jnp.float32)
    own = lax.dynamic_slice(places, (me, chan * rows), (1, rows))
    own = jnp.concatenate([own, own], axis=1)
    return pl.pallas_call(
        functools.partial(stack_kernel, nblk=count // TILE, scale=1.0 / math.sqrt(count)),
        out_shape=jax.ShapeDtypeStruct((rows, 3, 2 * LAGS), jnp.float32),
        in_specs=[SMEM] + [VMEM] * 4,
        out_specs=VMEM,
        scratch_shapes=scratch(rows, width) + [pltpu.VMEM(sums_shape(rows), jnp.float32)],
        compiler_params=PARAMS,
    )(targets, x, whole, places.reshape(sections, 1, count), own)


def place_row(pos_ref, q):
    every = pos_ref[...].astype(jnp.float32)
    at = lax.broadcasted_iota(jnp.int32, every.shape, 0)
    return jnp.sum(jnp.where(at == q, every, 0.0), axis=0, keepdims=True)


def half_row(row, half):
    return jnp.where(half == 0, row[:, :LANES], row[:, LANES:])


def twice(row, core):
    turned = pltpu.roll(row, LANES // 2, 1)
    low = lax.broadcasted_iota(jnp.int32, row.shape, 1) // (LANES // 2)
    return jnp.where(low == core, row, turned)


def where_am_i():
    me, chan = lax.axis_index("sect"), lax.axis_index("chan")
    return me, chan // 2, chan % 2


def own_kernel(x_ref, co_ref, yo_ref, cyo_ref, pos_ref, o_ref, t_ref, c_ref, w_ref, xs_ref, *, scale):
    me, half, core = where_am_i()
    rows = x_ref.shape[0]
    for flipped, ref in ((0, x_ref), (1, co_ref), (2, yo_ref), (3, cyo_ref)):
        at = ((2 * half + core) ^ flipped) * rows
        xs_ref[pl.ds(pl.multiple_of(at, rows), rows), :] = ref[...]
    build_windows(x_ref[...], t_ref)
    power = products(xs_ref[...], t_ref, c_ref)
    row = place_row(pos_ref, me)
    weigh(power, column_of(row), twice(half_row(row, half), core), w_ref, scale)

    def put(at, value):
        o_ref[at : at + 1, :] = value

    side_sums(c_ref, w_ref, 0, 4 * rows, put)


def pair_kernel(*refs, scale, across):
    partners_ref, x_ref = refs[:2]
    mine, peers = refs[2:5], refs[5:8]
    pos_ref, o_ref, t_ref, c_ref, w_ref, xs_ref = refs[8:]
    me, half, core = where_am_i()
    rows = x_ref.shape[0]
    whose = [partners_ref[k, me] for k in range(2)]
    for k in range(2):
        low = pl.multiple_of((2 * k + core) * rows, rows)
        high = pl.multiple_of((2 * k + 1 - core) * rows, rows)
        for away in range(3):

            @pl.when((whose[k] ^ me) == away + 1)
            def _():
                xs_ref[pl.ds(low, rows), :] = mine[away][...]
                xs_ref[pl.ds(high, rows), :] = peers[away][...]

    build_windows(x_ref[...], t_ref)
    power = products(xs_ref[...], t_ref, c_ref)
    columns = column_of(jnp.concatenate([half_row(place_row(pos_ref, q), half) for q in whose], axis=1))
    ours = half_row(place_row(pos_ref, me), 1 - half if across else half)
    weigh(power, columns, twice(ours, core), w_ref, scale)
    for k in range(2):

        def put(at, value):
            o_ref[k, at : at + 1, :] = value

        side_sums(c_ref, w_ref, 2 * rows * k, 2 * rows * (k + 1), put)


def join_kernel(own_ref, here_ref, there_ref, o_ref):
    rows = o_ref.shape[1]
    o_ref[0] = by_channel(own_ref[...], rows)
    for k in range(2):
        o_ref[1 + k] = by_channel(here_ref[k] + there_ref[k], rows)


def send(x, to):
    chans, sections = lax.axis_size("chan"), lax.axis_size("sect")
    pairs = []
    for c in range(chans):
        for s in range(sections):
            c2, s2 = to(c, s)
            pairs.append((c * sections + s, c2 * sections + s2))
    return lax.ppermute(x, ("chan", "sect"), pairs)


def stacks_by_flips(x, positions, partners):
    rows, width = x.shape
    scale = 1.0 / math.sqrt(4 * rows)
    z2 = send(x, lambda c, s: (c, s ^ 2))
    z3 = send(x, lambda c, s: (c, s ^ 3))
    z1 = send(x, lambda c, s: (c, s ^ 1))
    yo = send(x, lambda c, s: (c ^ 2, s))
    co = send(x, lambda c, s: (c ^ 1, s))
    co, yo, z1, z3, z2 = lax.optimization_barrier((co, yo, z1, z3, z2))
    cyo = send(yo, lambda c, s: (c ^ 1, s))
    cz1 = send(z1, lambda c, s: (c ^ 1, s))
    space = scratch(rows, width) + [pltpu.VMEM((4 * rows, width), jnp.bfloat16)]
    common = dict(out_specs=VMEM, compiler_params=PARAMS)
    own = pl.pallas_call(
        functools.partial(own_kernel, scale=scale),
        out_shape=jax.ShapeDtypeStruct(sums_shape(rows), jnp.float32),
        in_specs=[VMEM] * 5,
        scratch_shapes=space,
        **common,
    )(x, co, yo, cyo, positions)
    cz2 = send(z2, lambda c, s: (c ^ 1, s))
    cz3 = send(z3, lambda c, s: (c ^ 1, s))

    def pairs_of(source, across):
        return pl.pallas_call(
            functools.partial(pair_kernel, scale=scale, across=across),
            out_shape=jax.ShapeDtypeStruct(sums_shape(rows, 2), jnp.float32),
            in_specs=[SMEM] + [VMEM] * 8,
            scratch_shapes=space,
            **common,
        )(jnp.transpose(partners), source, z1, z2, z3, cz1, cz2, cz3, positions)

    there = send(pairs_of(yo, True), lambda c, s: (c ^ 2, s))
    here = pairs_of(x, False)
    stacks = pl.pallas_call(
        join_kernel,
        out_shape=jax.ShapeDtypeStruct((3, rows, 2 * LAGS), jnp.float32),
        in_specs=[VMEM] * 3,
        **common,
    )(own, here, there)
    return jnp.transpose(stacks, (1, 0, 2))


def body(traces, positions, partners):
    x = traces[0]
    me = lax.axis_index("sect")
    chan = lax.axis_index("chan")
    if lax.axis_size("chan") == 4 and lax.axis_size("sect") == 4:
        return stacks_by_flips(x, positions, partners)[None]
    targets = jnp.stack([me, partners[me, 0], partners[me, 1]])
    return stacks_anywhere(x, traces, positions, targets, me, chan)[None]


def solution(mesh):
    in_specs = (P(("days", "sect"), "chan", None), P(), P())
    out_specs = P(("days", "sect"), "chan", None, None)
    return jax.shard_map(body, mesh=mesh, in_specs=in_specs, out_specs=out_specs, check_vma=False)
```

time: 98.7 us -> 23.7 us (0.24); the launches traced: 97 us -> 23.5 us
  local copies, waits for them, and re-layouts: 68 us -> 0.69 us
  between operations: 17.8 us -> 0.06 us
  starting transfers between devices: 0.01 us -> 9.76 us
  Pallas kernels: 0 us -> 8.79 us
  matrix products: 6.24 us -> 0 us
  other arithmetic: 4.14 us -> 0 us
  waiting for transfers between devices: 0.73 us -> 4.18 us
    another operation x72 -> x0, local copies, waits for them, and re-layouts: 64.3 us -> none  [windows(): jnp.stack([padded[:, LAGS + half - lag_index:LAGS + half - lag_index + wi...]
    ppermute x0 -> x10, starting transfers between devices: none -> 9.76 us  [send(): return lax.ppermute(x, ('chan', 'sect'), pairs)]
    pallas_call x0 -> x4, Pallas kernels: none -> 8.79 us  [the longest x2 5.67 us: pairs_of(): pl.pallas_call(functools.partial(pair_kernel, scale=scale, across=across)...]
    dot_general x3 -> x0, matrix products: 6.24 us -> none  [section_terms(): lax.dot_general(flat, other, (((1,), (1,)), ((), ())), preferred_element_...]
    ppermute x0 -> x10, waiting for transfers between devices: none -> 4.18 us  [send(): return lax.ppermute(x, ('chan', 'sect'), pairs)]
    reduce_sum x2 -> x0, other arithmetic: 3.53 us -> none  [section_terms(): forward = jnp.sum(normed * ahead[:, None, :], axis=2)]
    dynamic_slice x2 -> x0, local copies, waits for them, and re-layouts: 1.43 us -> none  [the longest x1 1.42 us: body(): targets = (me_sect, partners[me_sect, 0], partners[me_sect, 1])]
    transpose x1 -> x0, local copies, waits for them, and re-layouts: 1.32 us -> none  [body(): whole.reshape(chan_size, sect_size, rows, whole.shape[2])]
  transfers between devices with their start and end apart: 1 -> 10, of which waited for: 0 -> 6; matrix products, arithmetic and copies ran while one was open for 68% -> 0% of each run, Pallas kernels for 0% -> 34%
where the time goes in v2:
time: 23.7 us; the launch traced here: 23.5 us
  starting transfers between devices  9.76 us (41%)
  Pallas kernels  8.79 us (37%)
  waiting for transfers between devices  4.18 us (18%)
  local copies, waits for them, and re-layouts  0.69 us (3%)
    ppermute x10, starting transfers between devices, send(): return lax.ppermute(x, ('chan', 'sect'), pairs)  9.76 us
    pallas_call x2, Pallas kernels, pairs_of(): pl.pallas_call(functools.partial(pair_kernel, scale=scale, across=across)...  5.67 us
    ppermute x10, waiting for transfers between devices, send(): return lax.ppermute(x, ('chan', 'sect'), pairs)  4.18 us
    pallas_call x1, Pallas kernels, stacks_by_flips(): pl.pallas_call(functools.partial(own_kernel, scale=scale), out_shape=jax....  2.24 us
    pallas_call x1, Pallas kernels, stacks_by_flips(): pl.pallas_call(join_kernel, out_shape=jax.ShapeDtypeStruct((3, rows, 2 *...  0.89 us
    unnamed x6, local copies, waits for them, and re-layouts  0.69 us
  transfers between devices with their start and end apart: 10, of which 6 were waited for; matrix products, arithmetic and copies ran while one was open for 0% of the time, Pallas kernels for 34%

profile of v2, /device:TPU:0, one launch (start us, length us, event | category | flops | bytes accessed | tf_op | source)
XLA Modules:
  0.0 23.5 jit_solution(11452588529712700497)
XLA Ops:
  0.0 4.0 %collective-permute-start.4 = (bf16[64,512]{1,0:T(8,128)(2,1)}, bf16[64,512]{1,0:T(8,128)(2,1)S(1)}, u32[]{:S(2)}, u32[]{:S(2)}) collective-permute-start(bf16[64,512]{1,0:T(8,128)(2,1)} %bitcast.5), channel_id=1, source_target_pairs={{0,2},{1,3},{2,0},{3,1},{4,6},{5,7},{6,4},{7,5},{8,10},{9,11},{10,... | collective-permute-start | bytes 196616 | tf_op jit(solution)/shard_map/ppermute | solution.py:220
  4.0 1.3 %collective-permute-start.3 = (bf16[64,512]{1,0:T(8,128)(2,1)}, bf16[64,512]{1,0:T(8,128)(2,1)S(1)}, u32[]{:S(2)}, u32[]{:S(2)}) collective-permute-start(bf16[64,512]{1,0:T(8,128)(2,1)} %bitcast.6), channel_id=1, source_target_pairs={{0,3},{1,2},{2,1},{3,0},{4,7},{5,6},{6,5},{7,4},{8,11},{9,10},{10,... | collective-permute-start | bytes 196616 | tf_op jit(solution)/shard_map/ppermute | solution.py:220
  5.4 0.2 collective-permute-start.2
  5.6 1.5 %collective-permute-start.1 = (bf16[64,512]{1,0:T(8,128)(2,1)}, bf16[64,512]{1,0:T(8,128)(2,1)S(1)}, u32[]{:S(2)}, u32[]{:S(2)}) collective-permute-start(bf16[64,512]{1,0:T(8,128)(2,1)} %bitcast.8), channel_id=1, source_target_pairs={{0,8},{1,9},{2,10},{3,11},{4,12},{5,13},{6,14},{7,15},{8,0},{9,1},... | collective-permute-start | bytes 196616 | tf_op jit(solution)/shard_map/ppermute | solution.py:220
  7.1 0.0 collective-permute-start
  7.1 0.9 %collective-permute-done.4.refs_3_ = bf16[64,512]{1,0:T(8,128)(2,1)S(1)} collective-permute-done((bf16[64,512]{1,0:T(8,128)(2,1)}, bf16[64,512]{1,0:T(8,128)(2,1)S(1)}, u32[]{:S(2)}, u32[]{:S(2)}) %collective-permute-start.4) | collective-permute-done | bytes 65568 | tf_op jit(solution)/shard_map/ppermute | solution.py:220
  8.0 2.5 %collective-permute-done.3.refs_4_ = bf16[64,512]{1,0:T(8,128)(2,1)S(1)} collective-permute-done((bf16[64,512]{1,0:T(8,128)(2,1)}, bf16[64,512]{1,0:T(8,128)(2,1)S(1)}, u32[]{:S(2)}, u32[]{:S(2)}) %collective-permute-start.3) | collective-permute-done | bytes 65568 | tf_op jit(solution)/shard_map/ppermute | solution.py:220
  10.5 0.1 collective-permute-done.2.refs_2_
  10.6 0.0 collective-permute-done.1.yo_ref.refs_1_
  10.6 0.0 collective-permute-start.6
  10.6 0.5 %collective-permute-start.7 = (bf16[64,512]{1,0:T(8,128)(2,1)S(1)}, bf16[64,512]{1,0:T(8,128)(2,1)S(1)}, u32[]{:S(2)}, u32[]{:S(2)}) collective-permute-start(bf16[64,512]{1,0:T(8,128)(2,1)S(1)} %collective-permute-done.4.refs_3_), channel_id=1, source_target_pairs={{0,4},{1,5},{2,6},{3,7},{4,0},{5,1},{6,2},{7,3},{8,12},{9,13},{10,... | collective-permute-start | bytes 196616 | tf_op jit(solution)/shard_map/ppermute | solution.py:220
  11.1 0.1 collective-permute-start.8
  11.2 0.4 %collective-permute-start.5 = (bf16[64,512]{1,0:T(8,128)(2,1)S(1)}, bf16[64,512]{1,0:T(8,128)(2,1)S(1)}, u32[]{:S(2)}, u32[]{:S(2)}) collective-permute-start(bf16[64,512]{1,0:T(8,128)(2,1)S(1)} %collective-permute-done.1.yo_ref.refs_1_), channel_id=1, source_target_pairs={{0,4},{1,5},{2,6},{3,7},{4,0},{5,1},{6,2},{7,3},{8,12},{9,13},{10,... | collective-permute-start | bytes 196616 | tf_op jit(solution)/shard_map/ppermute | solution.py:220
  11.6 0.2 collective-permute-done.6.refs_5_
  11.8 0.2 collective-permute-done.7.refs_6_
  12.0 0.4 %collective-permute-done.8.refs_7_ = bf16[64,512]{1,0:T(8,128)(2,1)S(1)} collective-permute-done((bf16[64,512]{1,0:T(8,128)(2,1)S(1)}, bf16[64,512]{1,0:T(8,128)(2,1)S(1)}, u32[]{:S(2)}, u32[]{:S(2)}) %collective-permute-start.8) | collective-permute-done | bytes 65568 | tf_op jit(solution)/shard_map/ppermute | solution.py:220
  12.4 0.7 %copy-done.1 = s32[4,256]{1,0:T(4,128)S(1)} copy-done((s32[4,256]{1,0:T(4,128)S(1)}, s32[4,256]{1,0:T(4,128)}, u32[]{:S(2)}) %copy-start.1) | copy-done | bytes 4120
  13.1 2.8 %shard_map.39 = f32[2,64,128]{2,1,0:T(8,128)S(1)} custom-call(s32[2,4]{1,0:T(2,128)S(1)} %bitcast.12, bf16[64,512]{1,0:T(8,128)(2,1)S(1)} %collective-permute-done.1.yo_ref.refs_1_, bf16[64,512]{1,0:T(8,128)(2,1)S(1)} %collective-permute-done.2.refs_2_, bf16[64,512]{1,0:T(8,128)(2,1)S(1)} %collective-permute-done.4.refs_3_, ...), custom_call_target="tpu_custom_call" | custom-call | tf_op jit(solution)/shard_map/pallas_call | solution.py:247
  15.9 1.6 %collective-permute-start.9 = (f32[2,64,128]{2,1,0:T(8,128)S(1)}, f32[2,64,128]{2,1,0:T(8,128)S(1)}, u32[]{:S(2)}, u32[]{:S(2)}) collective-permute-start(f32[2,64,128]{2,1,0:T(8,128)S(1)} %shard_map.39), channel_id=1, source_target_pairs={{0,8},{1,9},{2,10},{3,11},{4,12},{5,13},{6,14},{7,15},{8,0},{9,1},... | collective-permute-start | bytes 196616 | tf_op jit(solution)/shard_map/ppermute | solution.py:220
  17.5 2.8 %shard_map.38.here_ref = f32[2,64,128]{2,1,0:T(8,128)S(1)} custom-call(s32[2,4]{1,0:T(2,128)S(1)} %bitcast.13, bf16[64,512]{1,0:T(8,128)(2,1)S(1)} %bitcast.10, bf16[64,512]{1,0:T(8,128)(2,1)S(1)} %collective-permute-done.2.refs_2_, bf16[64,512]{1,0:T(8,128)(2,1)S(1)} %collective-permute-done.4.refs_3_, bf16[64,512]{1,0:T(8,128)(2,1)S(1)} %collective-permute-done.3.refs_4_, ...), custom_call_target="tpu_custom_call" | custom-call | tf_op jit(solution)/shard_map/pallas_call | solution.py:247
  20.3 0.0 collective-permute-done.5.cyo_ref
  20.3 2.2 %shard_map.37.own_ref = f32[64,128]{1,0:T(8,128)S(1)} custom-call(bf16[64,512]{1,0:T(8,128)(2,1)S(1)} %bitcast.11, bf16[64,512]{1,0:T(8,128)(2,1)S(1)} %collective-permute-done.co_ref, bf16[64,512]{1,0:T(8,128)(2,1)S(1)} %collective-permute-done.1.yo_ref.refs_1_, bf16[64,512]{1,0:T(8,128)(2,1)S(1)} %collective-permute-done.5.cyo_ref, s32[4,256]{1,0:T(4,128)S(1)} %copy-done.1), custom_call_target="tpu_custom_call" | custom-call | tf_op jit(solution)/shard_map/pallas_call | solution.py:236
  22.6 0.0 collective-permute-done.9.there_ref
  22.6 0.9 %shard_map.40 = f32[3,64,128]{2,1,0:T(8,128)} custom-call(f32[64,128]{1,0:T(8,128)S(1)} %shard_map.37.own_ref, f32[2,64,128]{2,1,0:T(8,128)S(1)} %shard_map.38.here_ref, f32[2,64,128]{2,1,0:T(8,128)S(1)} %collective-permute-done.9.there_ref), custom_call_target="tpu_custom_call" | custom-call | tf_op jit(solution)/shard_map/pallas_call | solution.py:257
  (6 shorter events, 0.0 us)
Async XLA Ops:
  0.0 12.4 %copy-start.2 = (s32[4,2]{0,1:T(2,128)S(1)}, s32[4,2]{0,1:T(2,128)}, u32[]{:S(2)}) copy-start(s32[4,2]{0,1:T(2,128)} %param.5) | copy-start | bytes 100
  0.0 8.0 %collective-permute-start.4 = (bf16[64,512]{1,0:T(8,128)(2,1)}, bf16[64,512]{1,0:T(8,128)(2,1)S(1)}, u32[]{:S(2)}, u32[]{:S(2)}) collective-permute-start(bf16[64,512]{1,0:T(8,128)(2,1)} %bitcast.5), channel_id=1, source_target_pairs={{0,2},{1,3},{2,0},{3,1},{4,6},{5,7},{6,4},{7,5},{8,10},{9,11},{10,... | collective-permute-start | bytes 196616 | tf_op jit(solution)/shard_map/ppermute | solution.py:220
  4.0 6.4 %collective-permute-start.3 = (bf16[64,512]{1,0:T(8,128)(2,1)}, bf16[64,512]{1,0:T(8,128)(2,1)S(1)}, u32[]{:S(2)}, u32[]{:S(2)}) collective-permute-start(bf16[64,512]{1,0:T(8,128)(2,1)} %bitcast.6), channel_id=1, source_target_pairs={{0,3},{1,2},{2,1},{3,0},{4,7},{5,6},{6,5},{7,4},{8,11},{9,10},{10,... | collective-permute-start | bytes 196616 | tf_op jit(solution)/shard_map/ppermute | solution.py:220
  5.4 5.2 %collective-permute-start.2 = (bf16[64,512]{1,0:T(8,128)(2,1)}, bf16[64,512]{1,0:T(8,128)(2,1)S(1)}, u32[]{:S(2)}, u32[]{:S(2)}) collective-permute-start(bf16[64,512]{1,0:T(8,128)(2,1)} %bitcast.7), channel_id=1, source_target_pairs={{0,1},{1,0},{2,3},{3,2},{4,5},{5,4},{6,7},{7,6},{8,9},{9,8},{10,11... | collective-permute-start | bytes 196616 | tf_op jit(solution)/shard_map/ppermute | solution.py:220
  5.6 5.0 %collective-permute-start.1 = (bf16[64,512]{1,0:T(8,128)(2,1)}, bf16[64,512]{1,0:T(8,128)(2,1)S(1)}, u32[]{:S(2)}, u32[]{:S(2)}) collective-permute-start(bf16[64,512]{1,0:T(8,128)(2,1)} %bitcast.8), channel_id=1, source_target_pairs={{0,8},{1,9},{2,10},{3,11},{4,12},{5,13},{6,14},{7,15},{8,0},{9,1},... | collective-permute-start | bytes 196616 | tf_op jit(solution)/shard_map/ppermute | solution.py:220
  7.1 3.4 %collective-permute-start = (bf16[64,512]{1,0:T(8,128)(2,1)}, bf16[64,512]{1,0:T(8,128)(2,1)S(1)}, u32[]{:S(2)}, u32[]{:S(2)}) collective-permute-start(bf16[64,512]{1,0:T(8,128)(2,1)} %bitcast.9), channel_id=1, source_target_pairs={{0,4},{1,5},{2,6},{3,7},{4,0},{5,1},{6,2},{7,3},{8,12},{9,13},{10,... | collective-permute-start | bytes 196616 | tf_op jit(solution)/shard_map/ppermute | solution.py:220
  10.6 1.3 %collective-permute-start.6 = (bf16[64,512]{1,0:T(8,128)(2,1)S(1)}, bf16[64,512]{1,0:T(8,128)(2,1)S(1)}, u32[]{:S(2)}, u32[]{:S(2)}) collective-permute-start(bf16[64,512]{1,0:T(8,128)(2,1)S(1)} %collective-permute-done.2.refs_2_), channel_id=1, source_target_pairs={{0,4},{1,5},{2,6},{3,7},{4,0},{5,1},{6,2},{7,3},{8,12},{9,13},{10,... | collective-permute-start | bytes 196616 | tf_op jit(solution)/shard_map/ppermute | solution.py:220
  10.6 1.4 %collective-permute-start.7 = (bf16[64,512]{1,0:T(8,128)(2,1)S(1)}, bf16[64,512]{1,0:T(8,128)(2,1)S(1)}, u32[]{:S(2)}, u32[]{:S(2)}) collective-permute-start(bf16[64,512]{1,0:T(8,128)(2,1)S(1)} %collective-permute-done.4.refs_3_), channel_id=1, source_target_pairs={{0,4},{1,5},{2,6},{3,7},{4,0},{5,1},{6,2},{7,3},{8,12},{9,13},{10,... | collective-permute-start | bytes 196616 | tf_op jit(solution)/shard_map/ppermute | solution.py:220
  11.1 1.3 %collective-permute-start.8 = (bf16[64,512]{1,0:T(8,128)(2,1)S(1)}, bf16[64,512]{1,0:T(8,128)(2,1)S(1)}, u32[]{:S(2)}, u32[]{:S(2)}) collective-permute-start(bf16[64,512]{1,0:T(8,128)(2,1)S(1)} %collective-permute-done.3.refs_4_), channel_id=1, source_target_pairs={{0,4},{1,5},{2,6},{3,7},{4,0},{5,1},{6,2},{7,3},{8,12},{9,13},{10,... | collective-permute-start | bytes 196616 | tf_op jit(solution)/shard_map/ppermute | solution.py:220
  11.2 9.1 %collective-permute-start.5 = (bf16[64,512]{1,0:T(8,128)(2,1)S(1)}, bf16[64,512]{1,0:T(8,128)(2,1)S(1)}, u32[]{:S(2)}, u32[]{:S(2)}) collective-permute-start(bf16[64,512]{1,0:T(8,128)(2,1)S(1)} %collective-permute-done.1.yo_ref.refs_1_), channel_id=1, source_target_pairs={{0,4},{1,5},{2,6},{3,7},{4,0},{5,1},{6,2},{7,3},{8,12},{9,13},{10,... | collective-permute-start | bytes 196616 | tf_op jit(solution)/shard_map/ppermute | solution.py:220
  12.4 0.7 %copy-start.1 = (s32[4,256]{1,0:T(4,128)S(1)}, s32[4,256]{1,0:T(4,128)}, u32[]{:S(2)}) copy-start(s32[4,256]{1,0:T(4,128)} %refs_8_.3) | copy-start | bytes 12292
  13.0 4.4 %copy-start = (bf16[1,64,512]{2,1,0:T(8,128)(2,1)S(1)}, bf16[1,64,512]{2,1,0:T(8,128)(2,1)}, u32[]{:S(2)}) copy-start(bf16[1,64,512]{2,1,0:T(8,128)(2,1)} %param.3) | copy-start | bytes 196612
  15.9 6.7 %collective-permute-start.9 = (f32[2,64,128]{2,1,0:T(8,128)S(1)}, f32[2,64,128]{2,1,0:T(8,128)S(1)}, u32[]{:S(2)}, u32[]{:S(2)}) collective-permute-start(f32[2,64,128]{2,1,0:T(8,128)S(1)} %shard_map.39), channel_id=1, source_target_pairs={{0,8},{1,9},{2,10},{3,11},{4,12},{5,13},{6,14},{7,15},{8,0},{9,1},... | collective-permute-start | bytes 196616 | tf_op jit(solution)/shard_map/ppermute | solution.py:220

commit v3 on v2

--- a/solution.py
+++ b/solution.py
@@ -156,51 +156,73 @@
     return me, chan // 2, chan % 2
 
 
-def own_kernel(x_ref, co_ref, yo_ref, cyo_ref, pos_ref, o_ref, t_ref, c_ref, w_ref, xs_ref, *, scale):
+def places_kernel(partners_ref, x_ref, pos_ref, xv_ref, rows_ref, cols_ref):
+    me, half, core = where_am_i()
+    xv_ref[...] = x_ref[...]
+    row = place_row(pos_ref, me)
+    rows_ref[0:1, :] = twice(half_row(row, half), core)
+    rows_ref[1:2, :] = twice(half_row(row, 1 - half), core)
+    whose = [partners_ref[k, me] for k in range(2)]
+    for k in range(2):
+        rows_ref[2 + k : 3 + k, :] = jnp.full((1, LANES), whose[k] ^ me, jnp.int32).astype(jnp.float32)
+    near = jnp.concatenate([half_row(place_row(pos_ref, q), half) for q in whose], axis=1)
+    cols_ref[0] = jnp.broadcast_to(column_of(near), cols_ref.shape[1:])
+    cols_ref[1] = jnp.broadcast_to(column_of(row), cols_ref.shape[1:])
+
+
+def gather_pairs(mine, peers, rows_ref, xs_ref, rows):
+    core = lax.axis_index("chan") % 2
+    for k in range(2):
+        away = rows_ref[2 + k : 3 + k, :]
+        picks = [(away == 1.0 + z).astype(jnp.bfloat16) for z in range(3)]
+        for w in range(xs_ref.shape[1] // LANES):
+            cut = slice(w * LANES, (w + 1) * LANES)
+            own = sum(ref[:, cut] * pick for ref, pick in zip(mine, picks))
+            peer = sum(peers[z * rows : (z + 1) * rows, cut] * pick for z, pick in enumerate(picks))
+            low = pl.multiple_of((2 * k + core) * rows, rows)
+            high = pl.multiple_of((2 * k + 1 - core) * rows, rows)
+            xs_ref[pl.ds(low, rows), cut] = own
+            xs_ref[pl.ds(high, rows), cut] = peer
+
+
+def pair_sums(xs_ref, t_ref, c_ref, w_ref, rows_ref, cols_ref, line, o_ref, rows, scale):
+    power = products(xs_ref[...], t_ref, c_ref)
+    weigh(power, cols_ref[0], rows_ref[line : line + 1, :], w_ref, scale)
+    for k in range(2):
+
+        def put(at, value):
+            o_ref[k, at : at + 1, :] = value
+
+        side_sums(c_ref, w_ref, 2 * rows * k, 2 * rows * (k + 1), put)
+
+
+def across_kernel(
+    yo_ref, z1_ref, z2_ref, z3_ref, cz_ref, rows_ref, cols_ref, o_ref, t_ref, c_ref, w_ref, xs_ref, *, scale
+):
+    rows = yo_ref.shape[0]
+    gather_pairs((z1_ref, z2_ref, z3_ref), cz_ref, rows_ref, xs_ref, rows)
+    build_windows(yo_ref[...], t_ref)
+    pair_sums(xs_ref, t_ref, c_ref, w_ref, rows_ref, cols_ref, 1, o_ref, rows, scale)
+
+
+def here_kernel(
+    x_ref, co_ref, yo_ref, cyo_ref, z1_ref, z2_ref, z3_ref, cz_ref, rows_ref, cols_ref, o_ref, own_ref, t_ref, c_ref, w_ref, xs_ref, *, scale
+):
     me, half, core = where_am_i()
     rows = x_ref.shape[0]
+    build_windows(x_ref[...], t_ref)
+    gather_pairs((z1_ref, z2_ref, z3_ref), cz_ref, rows_ref, xs_ref, rows)
+    pair_sums(xs_ref, t_ref, c_ref, w_ref, rows_ref, cols_ref, 0, o_ref, rows, scale)
     for flipped, ref in ((0, x_ref), (1, co_ref), (2, yo_ref), (3, cyo_ref)):
         at = ((2 * half + core) ^ flipped) * rows
         xs_ref[pl.ds(pl.multiple_of(at, rows), rows), :] = ref[...]
-    build_windows(x_ref[...], t_ref)
     power = products(xs_ref[...], t_ref, c_ref)
-    row = place_row(pos_ref, me)
-    weigh(power, column_of(row), twice(half_row(row, half), core), w_ref, scale)
+    weigh(power, cols_ref[1], rows_ref[0:1, :], w_ref, scale)
 
     def put(at, value):
-        o_ref[at : at + 1, :] = value
+        own_ref[at : at + 1, :] = value
 
     side_sums(c_ref, w_ref, 0, 4 * rows, put)
-
-
-def pair_kernel(*refs, scale, across):
-    partners_ref, x_ref = refs[:2]
-    mine, peers = refs[2:5], refs[5:8]
-    pos_ref, o_ref, t_ref, c_ref, w_ref, xs_ref = refs[8:]
-    me, half, core = where_am_i()
-    rows = x_ref.shape[0]
-    whose = [partners_ref[k, me] for k in range(2)]
-    for k in range(2):
-        low = pl.multiple_of((2 * k + core) * rows, rows)
-        high = pl.multiple_of((2 * k + 1 - core) * rows, rows)
-        for away in range(3):
-
-            @pl.when((whose[k] ^ me) == away + 1)
-            def _():
-                xs_ref[pl.ds(low, rows), :] = mine[away][...]
-                xs_ref[pl.ds(high, rows), :] = peers[away][...]
-
-    build_windows(x_ref[...], t_ref)
-    power = products(xs_ref[...], t_ref, c_ref)
-    columns = column_of(jnp.concatenate([half_row(place_row(pos_ref, q), half) for q in whose], axis=1))
-    ours = half_row(place_row(pos_ref, me), 1 - half if across else half)
-    weigh(power, columns, twice(ours, core), w_ref, scale)
-    for k in range(2):
-
-        def put(at, value):
-            o_ref[k, at : at + 1, :] = value
-
-        side_sums(c_ref, w_ref, 2 * rows * k, 2 * rows * (k + 1), put)
 
 
 def join_kernel(own_ref, here_ref, there_ref, o_ref):
@@ -223,42 +245,49 @@
 def stacks_by_flips(x, positions, partners):
     rows, width = x.shape
     scale = 1.0 / math.sqrt(4 * rows)
-    z2 = send(x, lambda c, s: (c, s ^ 2))
-    z3 = send(x, lambda c, s: (c, s ^ 3))
-    z1 = send(x, lambda c, s: (c, s ^ 1))
-    yo = send(x, lambda c, s: (c ^ 2, s))
-    co = send(x, lambda c, s: (c ^ 1, s))
-    co, yo, z1, z3, z2 = lax.optimization_barrier((co, yo, z1, z3, z2))
+    f32 = jnp.float32
+    xv, lines, columns = pl.pallas_call(
+        places_kernel,
+        out_shape=[
+            jax.ShapeDtypeStruct(x.shape, x.dtype),
+            jax.ShapeDtypeStruct((8, LANES), f32),
+            jax.ShapeDtypeStruct((2, 4 * rows, LANES), f32),
+        ],
+        in_specs=[SMEM] + [VMEM] * 2,
+        out_specs=[VMEM] * 3,
+        compiler_params=PARAMS,
+    )(jnp.transpose(partners), x, positions)
+    z1, z2, z3 = [send(x, lambda c, s: (c, s ^ k)) for k in (1, 2, 3)]
+    co, yo = [send(x, lambda c, s: (c ^ k, s)) for k in (1, 2)]
+    xv, lines, columns, z2, z3, z1, yo, co = lax.optimization_barrier((xv, lines, columns, z2, z3, z1, yo, co))
+    cz = send(jnp.concatenate([z1, z2, z3]), lambda c, s: (c ^ 1, s))
     cyo = send(yo, lambda c, s: (c ^ 1, s))
-    cz1 = send(z1, lambda c, s: (c ^ 1, s))
-    space = scratch(rows, width) + [pltpu.VMEM((4 * rows, width), jnp.bfloat16)]
-    common = dict(out_specs=VMEM, compiler_params=PARAMS)
-    own = pl.pallas_call(
-        functools.partial(own_kernel, scale=scale),
-        out_shape=jax.ShapeDtypeStruct(sums_shape(rows), jnp.float32),
-        in_specs=[VMEM] * 5,
+    space = scratch(rows, width) + [pltpu.VMEM((4 * rows, width), x.dtype)]
+    sums = jax.ShapeDtypeStruct(sums_shape(rows), f32)
+    pair = jax.ShapeDtypeStruct(sums_shape(rows, 2), f32)
+    across = pl.pallas_call(
+        functools.partial(across_kernel, scale=scale),
+        out_shape=pair,
+        in_specs=[VMEM] * 7,
+        out_specs=VMEM,
         scratch_shapes=space,
-        **common,
-    )(x, co, yo, cyo, positions)
-    cz2 = send(z2, lambda c, s: (c ^ 1, s))
-    cz3 = send(z3, lambda c, s: (c ^ 1, s))
-
-    def pairs_of(source, across):
-        return pl.pallas_call(
-            functools.partial(pair_kernel, scale=scale, across=across),
-            out_shape=jax.ShapeDtypeStruct(sums_shape(rows, 2), jnp.float32),
-            in_specs=[SMEM] + [VMEM] * 8,
-            scratch_shapes=space,
-            **common,
-        )(jnp.transpose(partners), source, z1, z2, z3, cz1, cz2, cz3, positions)
-
-    there = send(pairs_of(yo, True), lambda c, s: (c ^ 2, s))
-    here = pairs_of(x, False)
+        compiler_params=PARAMS,
+    )(yo, z1, z2, z3, cz, lines, columns)
+    there = send(across, lambda c, s: (c ^ 2, s))
+    here, own = pl.pallas_call(
+        functools.partial(here_kernel, scale=scale),
+        out_shape=[pair, sums],
+        in_specs=[VMEM] * 10,
+        out_specs=[VMEM] * 2,
+        scratch_shapes=space,
+        compiler_params=PARAMS,
+    )(xv, co, yo, cyo, z1, z2, z3, cz, lines, columns)
     stacks = pl.pallas_call(
         join_kernel,
-        out_shape=jax.ShapeDtypeStruct((3, rows, 2 * LAGS), jnp.float32),
+        out_shape=jax.ShapeDtypeStruct((3, rows, 2 * LAGS), f32),
         in_specs=[VMEM] * 3,
-        **common,
+        out_specs=VMEM,
+        compiler_params=PARAMS,
     )(own, here, there)
     return jnp.transpose(stacks, (1, 0, 2))
 

time: 23.7 us -> 20.9 us (0.88)
  waiting for transfers between devices: 4.18 us -> 1.92 us
  Pallas kernels: 8.79 us -> 7.88 us
  local copies, waits for them, and re-layouts: 0.69 us -> 1.56 us
  starting transfers between devices: 9.76 us -> 9.29 us
    ppermute x10 -> x8, waiting for transfers between devices: 4.18 us -> 1.92 us  [send(): return lax.ppermute(x, ('chan', 'sect'), pairs)]
    pallas_call x3, Pallas kernels: 7.9 us -> 6.99 us  [the longest x1 3.82 us: stacks_by_flips(): pl.pallas_call(functools.partial(here_kernel, scale=scale), out_shape=[pa...]
    unnamed x6, local copies, waits for them, and re-layouts: 0.69 us -> 1.56 us
    ppermute x10 -> x8, starting transfers between devices: 9.76 us -> 9.29 us  [send(): return lax.ppermute(x, ('chan', 'sect'), pairs)]
  transfers between devices with their start and end apart: 10 -> 8, of which waited for: 6 -> 3; matrix products, arithmetic and copies ran while one was open for 0% -> 0% of each run, Pallas kernels for 34% -> 34%
where the time goes in v3:
time: 20.9 us; the launch traced here: 20.7 us
  starting transfers between devices  9.29 us (44%)
  Pallas kernels  7.88 us (38%)
  waiting for transfers between devices  1.92 us (9%)
  local copies, waits for them, and re-layouts  1.56 us (7%)
    ppermute x8, starting transfers between devices, send(): return lax.ppermute(x, ('chan', 'sect'), pairs)  9.29 us
    pallas_call x1, Pallas kernels, stacks_by_flips(): pl.pallas_call(functools.partial(here_kernel, scale=scale), out_shape=[pa...  3.82 us
    pallas_call x1, Pallas kernels, stacks_by_flips(): pl.pallas_call(functools.partial(across_kernel, scale=scale), out_shape=p...  2.29 us
    ppermute x8, waiting for transfers between devices, send(): return lax.ppermute(x, ('chan', 'sect'), pairs)  1.92 us
    unnamed x6, local copies, waits for them, and re-layouts  1.56 us
    pallas_call x1, Pallas kernels, stacks_by_flips(): pl.pallas_call(join_kernel, out_shape=jax.ShapeDtypeStruct((3, rows, 2 *...  0.89 us
    pallas_call x1, Pallas kernels, stacks_by_flips(): pl.pallas_call(places_kernel, out_shape=[jax.ShapeDtypeStruct(x.shape, x....  0.88 us
  transfers between devices with their start and end apart: 8, of which 3 were waited for; matrix products, arithmetic and copies ran while one was open for 0% of the time, Pallas kernels for 34%

profile of v3, /device:TPU:0, one launch (start us, length us, event | category | flops | bytes accessed | tf_op | source)
XLA Modules:
  0.0 20.7 jit_solution(5202764431771556443)
XLA Ops:
  0.0 0.0 copy-start.2
  0.0 4.0 %collective-permute-start = (bf16[64,512]{1,0:T(8,128)(2,1)}, bf16[64,512]{1,0:T(8,128)(2,1)S(1)}, u32[]{:S(2)}, u32[]{:S(2)}) collective-permute-start(bf16[64,512]{1,0:T(8,128)(2,1)} %bitcast.5), channel_id=1, source_target_pairs={{0,2},{1,3},{2,0},{3,1},{4,6},{5,7},{6,4},{7,5},{8,10},{9,11},{10,... | collective-permute-start | bytes 196616 | tf_op jit(solution)/shard_map/ppermute | solution.py:242
  4.0 1.3 %collective-permute-start.1 = (bf16[64,512]{1,0:T(8,128)(2,1)}, bf16[64,512]{1,0:T(8,128)(2,1)S(1)}, u32[]{:S(2)}, u32[]{:S(2)}) collective-permute-start(bf16[64,512]{1,0:T(8,128)(2,1)} %bitcast.6), channel_id=1, source_target_pairs={{0,3},{1,2},{2,1},{3,0},{4,7},{5,6},{6,5},{7,4},{8,11},{9,10},{10,... | collective-permute-start | bytes 196616 | tf_op jit(solution)/shard_map/ppermute | solution.py:242
  5.4 0.2 %collective-permute-start.2 = (bf16[64,512]{1,0:T(8,128)(2,1)}, bf16[64,512]{1,0:T(8,128)(2,1)S(1)}, u32[]{:S(2)}, u32[]{:S(2)}) collective-permute-start(bf16[64,512]{1,0:T(8,128)(2,1)} %bitcast.7), channel_id=1, source_target_pairs={{0,1},{1,0},{2,3},{3,2},{4,5},{5,4},{6,7},{7,6},{8,9},{9,8},{10,11... | collective-permute-start | bytes 196616 | tf_op jit(solution)/shard_map/ppermute | solution.py:242
  5.6 1.5 %collective-permute-start.3 = (bf16[64,512]{1,0:T(8,128)(2,1)}, bf16[64,512]{1,0:T(8,128)(2,1)S(1)}, u32[]{:S(2)}, u32[]{:S(2)}) collective-permute-start(bf16[64,512]{1,0:T(8,128)(2,1)} %bitcast.8), channel_id=1, source_target_pairs={{0,8},{1,9},{2,10},{3,11},{4,12},{5,13},{6,14},{7,15},{8,0},{9,1},... | collective-permute-start | bytes 196616 | tf_op jit(solution)/shard_map/ppermute | solution.py:242
  7.1 0.0 collective-permute-start.4
  7.1 0.0 copy-done.2
  7.1 0.9 %copy-done = bf16[1,64,512]{2,1,0:T(8,128)(2,1)S(1)} copy-done((bf16[1,64,512]{2,1,0:T(8,128)(2,1)S(1)}, bf16[1,64,512]{2,1,0:T(8,128)(2,1)}, u32[]{:S(2)}) %copy-start) | copy-done | bytes 65560
  8.0 0.7 %copy-done.1 = s32[4,256]{1,0:T(4,128)S(1)} copy-done((s32[4,256]{1,0:T(4,128)S(1)}, s32[4,256]{1,0:T(4,128)}, u32[]{:S(2)}) %copy-start.1) | copy-done | bytes 4120
  8.7 0.9 %shard_map.37 = (bf16[64,512]{1,0:T(8,128)(2,1)S(1)}, f32[8,128]{1,0:T(8,128)S(1)}, f32[2,256,128]{2,1,0:T(8,128)S(1)}) custom-call(s32[2,4]{1,0:T(2,128)S(1)} %bitcast.11, bf16[64,512]{1,0:T(8,128)(2,1)S(1)} %bitcast.10, s32[4,256]{1,0:T(4,128)S(1)} %copy-done.1), custom_call_target="tpu_custom_call" | custom-call | tf_op jit(solution)/shard_map/pallas_call | solution.py:249
  9.6 0.0 collective-permute-done.z2_ref
  9.6 0.9 %collective-permute-done.1.z3_ref = bf16[64,512]{1,0:T(8,128)(2,1)S(1)} collective-permute-done((bf16[64,512]{1,0:T(8,128)(2,1)}, bf16[64,512]{1,0:T(8,128)(2,1)S(1)}, u32[]{:S(2)}, u32[]{:S(2)}) %collective-permute-start.1) | collective-permute-done | bytes 65568 | tf_op jit(solution)/shard_map/ppermute | solution.py:242
  10.5 0.1 collective-permute-done.2.z1_ref
  10.6 0.0 collective-permute-done.3.yo_ref
  10.6 0.0 collective-permute-done.4.co_ref
  10.6 0.1 collective-permute-start.6
  10.7 0.5 %collective-permute-start.5 = (bf16[64,512]{1,0:T(8,128)(2,1)S(1)}, bf16[64,512]{1,0:T(8,128)(2,1)S(1)}, u32[]{:S(2)}, u32[]{:S(2)}) collective-permute-start(bf16[64,512]{1,0:T(8,128)(2,1)S(1)} %collective-permute-done.3.yo_ref), channel_id=1, source_target_pairs={{0,4},{1,5},{2,6},{3,7},{4,0},{5,1},{6,2},{7,3},{8,12},{9,13},{10,... | collective-permute-start | bytes 196616 | tf_op jit(solution)/shard_map/ppermute | solution.py:242
  11.2 0.9 %collective-permute-done.6.cz_ref = bf16[192,512]{1,0:T(8,128)(2,1)S(1)} collective-permute-done((bf16[192,512]{1,0:T(8,128)(2,1)S(1)}, bf16[192,512]{1,0:T(8,128)(2,1)S(1)}, u32[]{:S(2)}, u32[]{:S(2)}) %collective-permute-start.6) | collective-permute-done | bytes 196640 | tf_op jit(solution)/shard_map/ppermute | solution.py:242
  12.1 2.3 %shard_map.39 = f32[2,64,128]{2,1,0:T(8,128)S(1)} custom-call(bf16[64,512]{1,0:T(8,128)(2,1)S(1)} %collective-permute-done.3.yo_ref, bf16[64,512]{1,0:T(8,128)(2,1)S(1)} %collective-permute-done.2.z1_ref, bf16[64,512]{1,0:T(8,128)(2,1)S(1)} %collective-permute-done.z2_ref, bf16[64,512]{1,0:T(8,128)(2,1)S(1)} %collective-permute-done.1.z3_ref, ...), custom_call_target="tpu_custom_call" | custom-call | tf_op jit(solution)/shard_map/pallas_call | solution.py:268
  14.4 1.6 %collective-permute-start.7 = (f32[2,64,128]{2,1,0:T(8,128)S(1)}, f32[2,64,128]{2,1,0:T(8,128)S(1)}, u32[]{:S(2)}, u32[]{:S(2)}) collective-permute-start(f32[2,64,128]{2,1,0:T(8,128)S(1)} %shard_map.39), channel_id=1, source_target_pairs={{0,8},{1,9},{2,10},{3,11},{4,12},{5,13},{6,14},{7,15},{8,0},{9,1},... | collective-permute-start | bytes 196616 | tf_op jit(solution)/shard_map/ppermute | solution.py:242
  16.0 0.0 collective-permute-done.5.cyo_ref
  16.0 3.8 %shard_map.38 = (f32[2,64,128]{2,1,0:T(8,128)S(1)}, f32[64,128]{1,0:T(8,128)S(1)}) custom-call(bf16[64,512]{1,0:T(8,128)(2,1)S(1)} %get-tuple-element.21.x_ref, bf16[64,512]{1,0:T(8,128)(2,1)S(1)} %collective-permute-done.4.co_ref, bf16[64,512]{1,0:T(8,128)(2,1)S(1)} %collective-permute-done.3.yo_ref, bf16[64,512]{1,0:T(8,128)(2,1)S(1)} %collective-permute-done.5.cyo_ref, ...), custom_call_target="tpu_custom_call" | custom-call | tf_op jit(solution)/shard_map/pallas_call | solution.py:277
  19.8 0.0 collective-permute-done.7.there_ref
  19.8 0.9 %shard_map.40 = f32[3,64,128]{2,1,0:T(8,128)} custom-call(f32[64,128]{1,0:T(8,128)S(1)} %get-tuple-element.29.own_ref, f32[2,64,128]{2,1,0:T(8,128)S(1)} %get-tuple-element.30.here_ref, f32[2,64,128]{2,1,0:T(8,128)S(1)} %collective-permute-done.7.there_ref), custom_call_target="tpu_custom_call" | custom-call | tf_op jit(solution)/shard_map/pallas_call | solution.py:285
  (3 shorter events, 0.0 us)
Async XLA Ops:
  0.0 7.1 %copy-start.2 = (s32[4,2]{0,1:T(2,128)S(1)}, s32[4,2]{0,1:T(2,128)}, u32[]{:S(2)}) copy-start(s32[4,2]{0,1:T(2,128)} %param.5) | copy-start | bytes 100
  0.0 9.6 %collective-permute-start = (bf16[64,512]{1,0:T(8,128)(2,1)}, bf16[64,512]{1,0:T(8,128)(2,1)S(1)}, u32[]{:S(2)}, u32[]{:S(2)}) collective-permute-start(bf16[64,512]{1,0:T(8,128)(2,1)} %bitcast.5), channel_id=1, source_target_pairs={{0,2},{1,3},{2,0},{3,1},{4,6},{5,7},{6,4},{7,5},{8,10},{9,11},{10,... | collective-permute-start | bytes 196616 | tf_op jit(solution)/shard_map/ppermute | solution.py:242
  4.0 6.4 %collective-permute-start.1 = (bf16[64,512]{1,0:T(8,128)(2,1)}, bf16[64,512]{1,0:T(8,128)(2,1)S(1)}, u32[]{:S(2)}, u32[]{:S(2)}) collective-permute-start(bf16[64,512]{1,0:T(8,128)(2,1)} %bitcast.6), channel_id=1, source_target_pairs={{0,3},{1,2},{2,1},{3,0},{4,7},{5,6},{6,5},{7,4},{8,11},{9,10},{10,... | collective-permute-start | bytes 196616 | tf_op jit(solution)/shard_map/ppermute | solution.py:242
  5.4 5.2 %collective-permute-start.2 = (bf16[64,512]{1,0:T(8,128)(2,1)}, bf16[64,512]{1,0:T(8,128)(2,1)S(1)}, u32[]{:S(2)}, u32[]{:S(2)}) collective-permute-start(bf16[64,512]{1,0:T(8,128)(2,1)} %bitcast.7), channel_id=1, source_target_pairs={{0,1},{1,0},{2,3},{3,2},{4,5},{5,4},{6,7},{7,6},{8,9},{9,8},{10,11... | collective-permute-start | bytes 196616 | tf_op jit(solution)/shard_map/ppermute | solution.py:242
  5.6 5.0 %collective-permute-start.3 = (bf16[64,512]{1,0:T(8,128)(2,1)}, bf16[64,512]{1,0:T(8,128)(2,1)S(1)}, u32[]{:S(2)}, u32[]{:S(2)}) collective-permute-start(bf16[64,512]{1,0:T(8,128)(2,1)} %bitcast.8), channel_id=1, source_target_pairs={{0,8},{1,9},{2,10},{3,11},{4,12},{5,13},{6,14},{7,15},{8,0},{9,1},... | collective-permute-start | bytes 196616 | tf_op jit(solution)/shard_map/ppermute | solution.py:242
  7.1 3.4 %collective-permute-start.4 = (bf16[64,512]{1,0:T(8,128)(2,1)}, bf16[64,512]{1,0:T(8,128)(2,1)S(1)}, u32[]{:S(2)}, u32[]{:S(2)}) collective-permute-start(bf16[64,512]{1,0:T(8,128)(2,1)} %bitcast.9), channel_id=1, source_target_pairs={{0,4},{1,5},{2,6},{3,7},{4,0},{5,1},{6,2},{7,3},{8,12},{9,13},{10,... | collective-permute-start | bytes 196616 | tf_op jit(solution)/shard_map/ppermute | solution.py:242
  7.1 0.9 %copy-start = (bf16[1,64,512]{2,1,0:T(8,128)(2,1)S(1)}, bf16[1,64,512]{2,1,0:T(8,128)(2,1)}, u32[]{:S(2)}) copy-start(bf16[1,64,512]{2,1,0:T(8,128)(2,1)} %param.3) | copy-start | bytes 196612
  8.0 0.7 %copy-start.1 = (s32[4,256]{1,0:T(4,128)S(1)}, s32[4,256]{1,0:T(4,128)}, u32[]{:S(2)}) copy-start(s32[4,256]{1,0:T(4,128)} %pos_ref.1) | copy-start | bytes 12292
  10.6 1.5 %collective-permute-start.6 = (bf16[192,512]{1,0:T(8,128)(2,1)S(1)}, bf16[192,512]{1,0:T(8,128)(2,1)S(1)}, u32[]{:S(2)}, u32[]{:S(2)}) collective-permute-start(bf16[192,512]{1,0:T(8,128)(2,1)S(1)} %pad_maximum_fusion), channel_id=1, source_target_pairs={{0,4},{1,5},{2,6},{3,7},{4,0},{5,1},{6,2},{7,3},{8,12},{9,13},{10,... | collective-permute-start | bytes 589832 | tf_op jit(solution)/shard_map/ppermute | solution.py:242
  10.7 5.3 %collective-permute-start.5 = (bf16[64,512]{1,0:T(8,128)(2,1)S(1)}, bf16[64,512]{1,0:T(8,128)(2,1)S(1)}, u32[]{:S(2)}, u32[]{:S(2)}) collective-permute-start(bf16[64,512]{1,0:T(8,128)(2,1)S(1)} %collective-permute-done.3.yo_ref), channel_id=1, source_target_pairs={{0,4},{1,5},{2,6},{3,7},{4,0},{5,1},{6,2},{7,3},{8,12},{9,13},{10,... | collective-permute-start | bytes 196616 | tf_op jit(solution)/shard_map/ppermute | solution.py:242
  14.4 5.4 %collective-permute-start.7 = (f32[2,64,128]{2,1,0:T(8,128)S(1)}, f32[2,64,128]{2,1,0:T(8,128)S(1)}, u32[]{:S(2)}, u32[]{:S(2)}) collective-permute-start(f32[2,64,128]{2,1,0:T(8,128)S(1)} %shard_map.39), channel_id=1, source_target_pairs={{0,8},{1,9},{2,10},{3,11},{4,12},{5,13},{6,14},{7,15},{8,0},{9,1},... | collective-permute-start | bytes 196616 | tf_op jit(solution)/shard_map/ppermute | solution.py:242

commit v4 on v3

--- a/solution.py
+++ b/solution.py
@@ -14,6 +14,7 @@
 TILE = 256
 VMEM = pl.BlockSpec(memory_space=pltpu.VMEM)
 SMEM = pl.BlockSpec(memory_space=pltpu.SMEM)
+HBM = pl.BlockSpec(memory_space=pltpu.MemorySpace.HBM)
 
 
 def build_windows(x, t_ref):
@@ -49,7 +50,7 @@
 
 
 def weigh(power, columns, own, w_ref, scale):
-    w = scale / jnp.sqrt(power * (1.0 / LAGS) + 1e-6)
+    w = scale * lax.rsqrt(power * (1.0 / LAGS) + 1e-6)
     ahead = columns >= own
     w_ref[0] = jnp.where(ahead, w, 0.0)
     w_ref[1] = jnp.where(ahead, 0.0, w)
@@ -156,18 +157,23 @@
     return me, chan // 2, chan % 2
 
 
-def places_kernel(partners_ref, x_ref, pos_ref, xv_ref, rows_ref, cols_ref):
+def places_kernel(partners_ref, x_ref, pos_ref, xv_ref, rows_ref, cols_ref, places_ref, sems):
     me, half, core = where_am_i()
-    xv_ref[...] = x_ref[...]
-    row = place_row(pos_ref, me)
+    get_x = pltpu.make_async_copy(x_ref, xv_ref, sems.at[0])
+    get_places = pltpu.make_async_copy(pos_ref, places_ref, sems.at[1])
+    get_x.start()
+    get_places.start()
+    get_places.wait()
+    row = place_row(places_ref, me)
     rows_ref[0:1, :] = twice(half_row(row, half), core)
     rows_ref[1:2, :] = twice(half_row(row, 1 - half), core)
     whose = [partners_ref[k, me] for k in range(2)]
     for k in range(2):
         rows_ref[2 + k : 3 + k, :] = jnp.full((1, LANES), whose[k] ^ me, jnp.int32).astype(jnp.float32)
-    near = jnp.concatenate([half_row(place_row(pos_ref, q), half) for q in whose], axis=1)
+    near = jnp.concatenate([half_row(place_row(places_ref, q), half) for q in whose], axis=1)
     cols_ref[0] = jnp.broadcast_to(column_of(near), cols_ref.shape[1:])
     cols_ref[1] = jnp.broadcast_to(column_of(row), cols_ref.shape[1:])
+    get_x.wait()
 
 
 def gather_pairs(mine, peers, rows_ref, xs_ref, rows):
@@ -253,10 +259,11 @@
             jax.ShapeDtypeStruct((8, LANES), f32),
             jax.ShapeDtypeStruct((2, 4 * rows, LANES), f32),
         ],
-        in_specs=[SMEM] + [VMEM] * 2,
+        in_specs=[SMEM, HBM, HBM],
         out_specs=[VMEM] * 3,
-        compiler_params=PARAMS,
-    )(jnp.transpose(partners), x, positions)
+        scratch_shapes=[pltpu.VMEM(positions.shape, positions.dtype), pltpu.SemaphoreType.DMA((2,))],
+        compiler_params=PARAMS,
+    )(jnp.transpose(partners), *[pltpu.with_memory_space_constraint(v, pltpu.MemorySpace.HBM) for v in (x, positions)])
     z1, z2, z3 = [send(x, lambda c, s: (c, s ^ k)) for k in (1, 2, 3)]
     co, yo = [send(x, lambda c, s: (c ^ k, s)) for k in (1, 2)]
     xv, lines, columns, z2, z3, z1, yo, co = lax.optimization_barrier((xv, lines, columns, z2, z3, z1, yo, co))

time: 20.9 us -> 20.7 us (level)
  local copies, waits for them, and re-layouts: 1.56 us -> 0.01 us
  waiting for transfers between devices: 1.92 us -> 2.71 us
  Pallas kernels: 7.88 us -> 8.49 us
    unnamed x6 -> x2, local copies, waits for them, and re-layouts: 1.56 us -> 0.01 us
    ppermute x8, waiting for transfers between devices: 1.92 us -> 2.71 us  [send(): return lax.ppermute(x, ('chan', 'sect'), pairs)]
    pallas_call x1, Pallas kernels: 0.88 us -> 1.64 us  [stacks_by_flips(): pl.pallas_call(places_kernel, out_shape=[jax.ShapeDtypeStruct(x.shape, x....]
  transfers between devices with their start and end apart: 8 -> 8, of which waited for: 3 -> 3; matrix products, arithmetic and copies ran while one was open for 0% -> 0% of each run, Pallas kernels for 34% -> 37%
where the time goes in v4:
time: 20.7 us; the launch traced here: 20.6 us
  starting transfers between devices  9.29 us (45%)
  Pallas kernels  8.49 us (41%)
  waiting for transfers between devices  2.71 us (13%)
    ppermute x8, starting transfers between devices, send(): return lax.ppermute(x, ('chan', 'sect'), pairs)  9.29 us
    pallas_call x1, Pallas kernels, stacks_by_flips(): pl.pallas_call(functools.partial(here_kernel, scale=scale), out_shape=[pa...  3.71 us
    ppermute x8, waiting for transfers between devices, send(): return lax.ppermute(x, ('chan', 'sect'), pairs)  2.71 us
    pallas_call x1, Pallas kernels, stacks_by_flips(): pl.pallas_call(functools.partial(across_kernel, scale=scale), out_shape=p...  2.25 us
    pallas_call x1, Pallas kernels, stacks_by_flips(): pl.pallas_call(places_kernel, out_shape=[jax.ShapeDtypeStruct(x.shape, x....  1.64 us
    pallas_call x1, Pallas kernels, stacks_by_flips(): pl.pallas_call(join_kernel, out_shape=jax.ShapeDtypeStruct((3, rows, 2 *...  0.89 us
  transfers between devices with their start and end apart: 8, of which 3 were waited for; matrix products, arithmetic and copies ran while one was open for 0% of the time, Pallas kernels for 37%

profile of v4, /device:TPU:0, one launch (start us, length us, event | category | flops | bytes accessed | tf_op | source)
XLA Modules:
  0.0 20.6 jit_solution(365589794296183002)
XLA Ops:
  0.0 0.0 copy-start
  0.0 4.0 %collective-permute-start = (bf16[64,512]{1,0:T(8,128)(2,1)}, bf16[64,512]{1,0:T(8,128)(2,1)S(1)}, u32[]{:S(2)}, u32[]{:S(2)}) collective-permute-start(bf16[64,512]{1,0:T(8,128)(2,1)} %bitcast.6), channel_id=1, source_target_pairs={{0,2},{1,3},{2,0},{3,1},{4,6},{5,7},{6,4},{7,5},{8,10},{9,11},{10,... | collective-permute-start | bytes 196616 | tf_op jit(solution)/shard_map/ppermute | solution.py:248
  4.0 1.3 %collective-permute-start.1 = (bf16[64,512]{1,0:T(8,128)(2,1)}, bf16[64,512]{1,0:T(8,128)(2,1)S(1)}, u32[]{:S(2)}, u32[]{:S(2)}) collective-permute-start(bf16[64,512]{1,0:T(8,128)(2,1)} %bitcast.7), channel_id=1, source_target_pairs={{0,3},{1,2},{2,1},{3,0},{4,7},{5,6},{6,5},{7,4},{8,11},{9,10},{10,... | collective-permute-start | bytes 196616 | tf_op jit(solution)/shard_map/ppermute | solution.py:248
  5.4 0.2 %collective-permute-start.2 = (bf16[64,512]{1,0:T(8,128)(2,1)}, bf16[64,512]{1,0:T(8,128)(2,1)S(1)}, u32[]{:S(2)}, u32[]{:S(2)}) collective-permute-start(bf16[64,512]{1,0:T(8,128)(2,1)} %bitcast.8), channel_id=1, source_target_pairs={{0,1},{1,0},{2,3},{3,2},{4,5},{5,4},{6,7},{7,6},{8,9},{9,8},{10,11... | collective-permute-start | bytes 196616 | tf_op jit(solution)/shard_map/ppermute | solution.py:248
  5.6 1.5 %collective-permute-start.3 = (bf16[64,512]{1,0:T(8,128)(2,1)}, bf16[64,512]{1,0:T(8,128)(2,1)S(1)}, u32[]{:S(2)}, u32[]{:S(2)}) collective-permute-start(bf16[64,512]{1,0:T(8,128)(2,1)} %bitcast.9), channel_id=1, source_target_pairs={{0,8},{1,9},{2,10},{3,11},{4,12},{5,13},{6,14},{7,15},{8,0},{9,1},... | collective-permute-start | bytes 196616 | tf_op jit(solution)/shard_map/ppermute | solution.py:248
  7.1 0.0 collective-permute-start.4
  7.1 0.0 copy-done
  7.1 1.6 %shard_map.37 = (bf16[64,512]{1,0:T(8,128)(2,1)S(1)}, f32[8,128]{1,0:T(8,128)S(1)}, f32[2,256,128]{2,1,0:T(8,128)S(1)}) custom-call(s32[2,4]{1,0:T(2,128)S(1)} %bitcast.5, bf16[64,512]{1,0:T(8,128)(2,1)} %bitcast.11, s32[4,256]{1,0:T(4,128)} %pos_ref.1), custom_call_target="tpu_custom_call" | custom-call | tf_op jit(solution)/shard_map/pallas_call | solution.py:255
  8.8 0.0 collective-permute-done.z2_ref
  8.8 1.7 %collective-permute-done.1.z3_ref = bf16[64,512]{1,0:T(8,128)(2,1)S(1)} collective-permute-done((bf16[64,512]{1,0:T(8,128)(2,1)}, bf16[64,512]{1,0:T(8,128)(2,1)S(1)}, u32[]{:S(2)}, u32[]{:S(2)}) %collective-permute-start.1) | collective-permute-done | bytes 65568 | tf_op jit(solution)/shard_map/ppermute | solution.py:248
  10.5 0.1 collective-permute-done.2.z1_ref
  10.6 0.0 collective-permute-done.3.yo_ref
  10.6 0.0 collective-permute-done.4.co_ref
  10.6 0.1 collective-permute-start.6
  10.7 0.5 %collective-permute-start.5 = (bf16[64,512]{1,0:T(8,128)(2,1)S(1)}, bf16[64,512]{1,0:T(8,128)(2,1)S(1)}, u32[]{:S(2)}, u32[]{:S(2)}) collective-permute-start(bf16[64,512]{1,0:T(8,128)(2,1)S(1)} %collective-permute-done.3.yo_ref), channel_id=1, source_target_pairs={{0,4},{1,5},{2,6},{3,7},{4,0},{5,1},{6,2},{7,3},{8,12},{9,13},{10,... | collective-permute-start | bytes 196616 | tf_op jit(solution)/shard_map/ppermute | solution.py:248
  11.2 0.9 %collective-permute-done.6.cz_ref = bf16[192,512]{1,0:T(8,128)(2,1)S(1)} collective-permute-done((bf16[192,512]{1,0:T(8,128)(2,1)S(1)}, bf16[192,512]{1,0:T(8,128)(2,1)S(1)}, u32[]{:S(2)}, u32[]{:S(2)}) %collective-permute-start.6) | collective-permute-done | bytes 196640 | tf_op jit(solution)/shard_map/ppermute | solution.py:248
  12.1 2.3 %shard_map.39 = f32[2,64,128]{2,1,0:T(8,128)S(1)} custom-call(bf16[64,512]{1,0:T(8,128)(2,1)S(1)} %collective-permute-done.3.yo_ref, bf16[64,512]{1,0:T(8,128)(2,1)S(1)} %collective-permute-done.2.z1_ref, bf16[64,512]{1,0:T(8,128)(2,1)S(1)} %collective-permute-done.z2_ref, bf16[64,512]{1,0:T(8,128)(2,1)S(1)} %collective-permute-done.1.z3_ref, ...), custom_call_target="tpu_custom_call" | custom-call | tf_op jit(solution)/shard_map/pallas_call | solution.py:275
  14.4 1.6 %collective-permute-start.7 = (f32[2,64,128]{2,1,0:T(8,128)S(1)}, f32[2,64,128]{2,1,0:T(8,128)S(1)}, u32[]{:S(2)}, u32[]{:S(2)}) collective-permute-start(f32[2,64,128]{2,1,0:T(8,128)S(1)} %shard_map.39), channel_id=1, source_target_pairs={{0,8},{1,9},{2,10},{3,11},{4,12},{5,13},{6,14},{7,15},{8,0},{9,1},... | collective-permute-start | bytes 196616 | tf_op jit(solution)/shard_map/ppermute | solution.py:248
  15.9 0.0 collective-permute-done.5.cyo_ref
  15.9 3.7 %shard_map.38 = (f32[2,64,128]{2,1,0:T(8,128)S(1)}, f32[64,128]{1,0:T(8,128)S(1)}) custom-call(bf16[64,512]{1,0:T(8,128)(2,1)S(1)} %get-tuple-element.21.x_ref, bf16[64,512]{1,0:T(8,128)(2,1)S(1)} %collective-permute-done.4.co_ref, bf16[64,512]{1,0:T(8,128)(2,1)S(1)} %collective-permute-done.3.yo_ref, bf16[64,512]{1,0:T(8,128)(2,1)S(1)} %collective-permute-done.5.cyo_ref, ...), custom_call_target="tpu_custom_call" | custom-call | tf_op jit(solution)/shard_map/pallas_call | solution.py:284
  19.7 0.0 collective-permute-done.7.there_ref
  19.7 0.9 %shard_map.40 = f32[3,64,128]{2,1,0:T(8,128)} custom-call(f32[64,128]{1,0:T(8,128)S(1)} %get-tuple-element.29.own_ref, f32[2,64,128]{2,1,0:T(8,128)S(1)} %get-tuple-element.30.here_ref, f32[2,64,128]{2,1,0:T(8,128)S(1)} %collective-permute-done.7.there_ref), custom_call_target="tpu_custom_call" | custom-call | tf_op jit(solution)/shard_map/pallas_call | solution.py:292
  (1 shorter events, 0.0 us)
Async XLA Ops:
  0.0 7.1 %copy-start = (s32[4,2]{0,1:T(2,128)S(1)}, s32[4,2]{0,1:T(2,128)}, u32[]{:S(2)}) copy-start(s32[4,2]{0,1:T(2,128)} %param.5) | copy-start | bytes 100
  0.0 8.8 %collective-permute-start = (bf16[64,512]{1,0:T(8,128)(2,1)}, bf16[64,512]{1,0:T(8,128)(2,1)S(1)}, u32[]{:S(2)}, u32[]{:S(2)}) collective-permute-start(bf16[64,512]{1,0:T(8,128)(2,1)} %bitcast.6), channel_id=1, source_target_pairs={{0,2},{1,3},{2,0},{3,1},{4,6},{5,7},{6,4},{7,5},{8,10},{9,11},{10,... | collective-permute-start | bytes 196616 | tf_op jit(solution)/shard_map/ppermute | solution.py:248
  4.0 6.4 %collective-permute-start.1 = (bf16[64,512]{1,0:T(8,128)(2,1)}, bf16[64,512]{1,0:T(8,128)(2,1)S(1)}, u32[]{:S(2)}, u32[]{:S(2)}) collective-permute-start(bf16[64,512]{1,0:T(8,128)(2,1)} %bitcast.7), channel_id=1, source_target_pairs={{0,3},{1,2},{2,1},{3,0},{4,7},{5,6},{6,5},{7,4},{8,11},{9,10},{10,... | collective-permute-start | bytes 196616 | tf_op jit(solution)/shard_map/ppermute | solution.py:248
  5.4 5.2 %collective-permute-start.2 = (bf16[64,512]{1,0:T(8,128)(2,1)}, bf16[64,512]{1,0:T(8,128)(2,1)S(1)}, u32[]{:S(2)}, u32[]{:S(2)}) collective-permute-start(bf16[64,512]{1,0:T(8,128)(2,1)} %bitcast.8), channel_id=1, source_target_pairs={{0,1},{1,0},{2,3},{3,2},{4,5},{5,4},{6,7},{7,6},{8,9},{9,8},{10,11... | collective-permute-start | bytes 196616 | tf_op jit(solution)/shard_map/ppermute | solution.py:248
  5.6 5.0 %collective-permute-start.3 = (bf16[64,512]{1,0:T(8,128)(2,1)}, bf16[64,512]{1,0:T(8,128)(2,1)S(1)}, u32[]{:S(2)}, u32[]{:S(2)}) collective-permute-start(bf16[64,512]{1,0:T(8,128)(2,1)} %bitcast.9), channel_id=1, source_target_pairs={{0,8},{1,9},{2,10},{3,11},{4,12},{5,13},{6,14},{7,15},{8,0},{9,1},... | collective-permute-start | bytes 196616 | tf_op jit(solution)/shard_map/ppermute | solution.py:248
  7.1 3.4 %collective-permute-start.4 = (bf16[64,512]{1,0:T(8,128)(2,1)}, bf16[64,512]{1,0:T(8,128)(2,1)S(1)}, u32[]{:S(2)}, u32[]{:S(2)}) collective-permute-start(bf16[64,512]{1,0:T(8,128)(2,1)} %bitcast.10), channel_id=1, source_target_pairs={{0,4},{1,5},{2,6},{3,7},{4,0},{5,1},{6,2},{7,3},{8,12},{9,13},{10,... | collective-permute-start | bytes 196616 | tf_op jit(solution)/shard_map/ppermute | solution.py:248
  10.6 1.5 %collective-permute-start.6 = (bf16[192,512]{1,0:T(8,128)(2,1)S(1)}, bf16[192,512]{1,0:T(8,128)(2,1)S(1)}, u32[]{:S(2)}, u32[]{:S(2)}) collective-permute-start(bf16[192,512]{1,0:T(8,128)(2,1)S(1)} %pad_maximum_fusion), channel_id=1, source_target_pairs={{0,4},{1,5},{2,6},{3,7},{4,0},{5,1},{6,2},{7,3},{8,12},{9,13},{10,... | collective-permute-start | bytes 589832 | tf_op jit(solution)/shard_map/ppermute | solution.py:248
  10.7 5.3 %collective-permute-start.5 = (bf16[64,512]{1,0:T(8,128)(2,1)S(1)}, bf16[64,512]{1,0:T(8,128)(2,1)S(1)}, u32[]{:S(2)}, u32[]{:S(2)}) collective-permute-start(bf16[64,512]{1,0:T(8,128)(2,1)S(1)} %collective-permute-done.3.yo_ref), channel_id=1, source_target_pairs={{0,4},{1,5},{2,6},{3,7},{4,0},{5,1},{6,2},{7,3},{8,12},{9,13},{10,... | collective-permute-start | bytes 196616 | tf_op jit(solution)/shard_map/ppermute | solution.py:248
  14.4 5.3 %collective-permute-start.7 = (f32[2,64,128]{2,1,0:T(8,128)S(1)}, f32[2,64,128]{2,1,0:T(8,128)S(1)}, u32[]{:S(2)}, u32[]{:S(2)}) collective-permute-start(f32[2,64,128]{2,1,0:T(8,128)S(1)} %shard_map.39), channel_id=1, source_target_pairs={{0,8},{1,9},{2,10},{3,11},{4,12},{5,13},{6,14},{7,15},{8,0},{9,1},... | collective-permute-start | bytes 196616 | tf_op jit(solution)/shard_map/ppermute | solution.py:248

commit v5 on v4

--- a/solution.py
+++ b/solution.py
@@ -101,11 +101,11 @@
         o_ref[:, k, :] = by_channel(acc_ref[...], rows)
 
 
-def scratch(rows, width):
+def scratch(rows, width, count):
     return [
         pltpu.VMEM((LAGS * rows, width), jnp.bfloat16),
-        pltpu.VMEM((TILE, LAGS * rows), jnp.float32),
-        pltpu.VMEM((2, TILE, LANES), jnp.float32),
+        pltpu.VMEM((count, LAGS * rows), jnp.float32),
+        pltpu.VMEM((2, count, LANES), jnp.float32),
     ]
 
 
@@ -131,7 +131,7 @@
         out_shape=jax.ShapeDtypeStruct((rows, 3, 2 * LAGS), jnp.float32),
         in_specs=[SMEM] + [VMEM] * 4,
         out_specs=VMEM,
-        scratch_shapes=scratch(rows, width) + [pltpu.VMEM(sums_shape(rows), jnp.float32)],
+        scratch_shapes=scratch(rows, width, TILE) + [pltpu.VMEM(sums_shape(rows), jnp.float32)],
         compiler_params=PARAMS,
     )(targets, x, whole, places.reshape(sections, 1, count), own)
 
@@ -157,23 +157,40 @@
     return me, chan // 2, chan % 2
 
 
-def places_kernel(partners_ref, x_ref, pos_ref, xv_ref, rows_ref, cols_ref, places_ref, sems):
+def first_kernel(
+    partners_ref, x_ref, pos_ref, xv_ref, rows_ref, cols_ref, o_ref, t_ref, c_ref, w_ref, places_ref, sems, *, scale
+):
     me, half, core = where_am_i()
+    rows = x_ref.shape[0]
     get_x = pltpu.make_async_copy(x_ref, xv_ref, sems.at[0])
     get_places = pltpu.make_async_copy(pos_ref, places_ref, sems.at[1])
     get_x.start()
     get_places.start()
     get_places.wait()
     row = place_row(places_ref, me)
-    rows_ref[0:1, :] = twice(half_row(row, half), core)
-    rows_ref[1:2, :] = twice(half_row(row, 1 - half), core)
+    ours = twice(half_row(row, half), core)
+    across = twice(half_row(row, 1 - half), core)
+    rows_ref[0:1, :] = ours
+    rows_ref[1:2, :] = across
     whose = [partners_ref[k, me] for k in range(2)]
     for k in range(2):
         rows_ref[2 + k : 3 + k, :] = jnp.full((1, LANES), whose[k] ^ me, jnp.int32).astype(jnp.float32)
-    near = jnp.concatenate([half_row(place_row(places_ref, q), half) for q in whose], axis=1)
-    cols_ref[0] = jnp.broadcast_to(column_of(near), cols_ref.shape[1:])
-    cols_ref[1] = jnp.broadcast_to(column_of(row), cols_ref.shape[1:])
+        near = column_of(half_row(place_row(places_ref, whose[k]), half))
+        cols_ref[2 * rows * k : 2 * rows * (k + 1), :] = jnp.broadcast_to(near, (2 * rows, LANES))
+    others = (twice(half_row(row, half), 1 - core), across, twice(half_row(row, 1 - half), 1 - core))
+    for k, other in enumerate(others):
+        at = slice((4 + k) * rows, (5 + k) * rows)
+        cols_ref[at, :] = jnp.broadcast_to(column_of(other)[:rows], (rows, LANES))
     get_x.wait()
+    x = xv_ref[...]
+    build_windows(x, t_ref)
+    power = products(x, t_ref, c_ref)
+    weigh(power, column_of(ours)[:rows], ours, w_ref, scale)
+
+    def put(at, value):
+        o_ref[at : at + 1, :] = value
+
+    side_sums(c_ref, w_ref, 0, rows, put)
 
 
 def gather_pairs(mine, peers, rows_ref, xs_ref, rows):
@@ -191,49 +208,44 @@
             xs_ref[pl.ds(high, rows), cut] = peer
 
 
-def pair_sums(xs_ref, t_ref, c_ref, w_ref, rows_ref, cols_ref, line, o_ref, rows, scale):
+def target_sums(xs_ref, t_ref, c_ref, w_ref, ours, cols_ref, o_ref, scale):
+    count = xs_ref.shape[0]
     power = products(xs_ref[...], t_ref, c_ref)
-    weigh(power, cols_ref[0], rows_ref[line : line + 1, :], w_ref, scale)
-    for k in range(2):
+    weigh(power, cols_ref[0:count, :], ours, w_ref, scale)
+    edges = [e for e in (0, LANES, 2 * LANES, count) if e <= count]
+    for k, (low, high) in enumerate(zip(edges[:-1], edges[1:])):
+        if low == high:
+            continue
 
         def put(at, value):
             o_ref[k, at : at + 1, :] = value
 
-        side_sums(c_ref, w_ref, 2 * rows * k, 2 * rows * (k + 1), put)
+        side_sums(c_ref, w_ref, low, high, put)
 
 
 def across_kernel(
     yo_ref, z1_ref, z2_ref, z3_ref, cz_ref, rows_ref, cols_ref, o_ref, t_ref, c_ref, w_ref, xs_ref, *, scale
 ):
     rows = yo_ref.shape[0]
+    build_windows(yo_ref[...], t_ref)
     gather_pairs((z1_ref, z2_ref, z3_ref), cz_ref, rows_ref, xs_ref, rows)
-    build_windows(yo_ref[...], t_ref)
-    pair_sums(xs_ref, t_ref, c_ref, w_ref, rows_ref, cols_ref, 1, o_ref, rows, scale)
+    target_sums(xs_ref, t_ref, c_ref, w_ref, rows_ref[1:2, :], cols_ref, o_ref, scale)
 
 
 def here_kernel(
-    x_ref, co_ref, yo_ref, cyo_ref, z1_ref, z2_ref, z3_ref, cz_ref, rows_ref, cols_ref, o_ref, own_ref, t_ref, c_ref, w_ref, xs_ref, *, scale
+    x_ref, co_ref, yo_ref, cyo_ref, z1_ref, z2_ref, z3_ref, cz_ref, rows_ref, cols_ref, o_ref, t_ref, c_ref, w_ref, xs_ref, *, scale
 ):
-    me, half, core = where_am_i()
     rows = x_ref.shape[0]
     build_windows(x_ref[...], t_ref)
     gather_pairs((z1_ref, z2_ref, z3_ref), cz_ref, rows_ref, xs_ref, rows)
-    pair_sums(xs_ref, t_ref, c_ref, w_ref, rows_ref, cols_ref, 0, o_ref, rows, scale)
-    for flipped, ref in ((0, x_ref), (1, co_ref), (2, yo_ref), (3, cyo_ref)):
-        at = ((2 * half + core) ^ flipped) * rows
-        xs_ref[pl.ds(pl.multiple_of(at, rows), rows), :] = ref[...]
-    power = products(xs_ref[...], t_ref, c_ref)
-    weigh(power, cols_ref[1], rows_ref[0:1, :], w_ref, scale)
-
-    def put(at, value):
-        own_ref[at : at + 1, :] = value
-
-    side_sums(c_ref, w_ref, 0, 4 * rows, put)
+    for k, ref in enumerate((co_ref, yo_ref, cyo_ref)):
+        xs_ref[(4 + k) * rows : (5 + k) * rows, :] = ref[...]
+    target_sums(xs_ref, t_ref, c_ref, w_ref, rows_ref[0:1, :], cols_ref, o_ref, scale)
 
 
 def join_kernel(own_ref, here_ref, there_ref, o_ref):
     rows = o_ref.shape[1]
-    o_ref[0] = by_channel(own_ref[...], rows)
+    o_ref[0] = by_channel(own_ref[...] + here_ref[2], rows)
     for k in range(2):
         o_ref[1 + k] = by_channel(here_ref[k] + there_ref[k], rows)
 
@@ -251,51 +263,51 @@
 def stacks_by_flips(x, positions, partners):
     rows, width = x.shape
     scale = 1.0 / math.sqrt(4 * rows)
-    f32 = jnp.float32
-    xv, lines, columns = pl.pallas_call(
-        places_kernel,
+    sums = lambda *count: jax.ShapeDtypeStruct(sums_shape(rows, *count), jnp.float32)
+    space = lambda blocks: scratch(rows, width, blocks * rows) + [pltpu.VMEM((blocks * rows, width), x.dtype)]
+    xv, lines, columns, near = pl.pallas_call(
+        functools.partial(first_kernel, scale=scale),
         out_shape=[
             jax.ShapeDtypeStruct(x.shape, x.dtype),
-            jax.ShapeDtypeStruct((8, LANES), f32),
-            jax.ShapeDtypeStruct((2, 4 * rows, LANES), f32),
+            jax.ShapeDtypeStruct((8, LANES), jnp.float32),
+            jax.ShapeDtypeStruct((7 * rows, LANES), jnp.float32),
+            sums(),
         ],
         in_specs=[SMEM, HBM, HBM],
-        out_specs=[VMEM] * 3,
-        scratch_shapes=[pltpu.VMEM(positions.shape, positions.dtype), pltpu.SemaphoreType.DMA((2,))],
+        out_specs=[VMEM] * 4,
+        scratch_shapes=scratch(rows, width, rows)
+        + [pltpu.VMEM(positions.shape, positions.dtype), pltpu.SemaphoreType.DMA((2,))],
         compiler_params=PARAMS,
     )(jnp.transpose(partners), *[pltpu.with_memory_space_constraint(v, pltpu.MemorySpace.HBM) for v in (x, positions)])
     z1, z2, z3 = [send(x, lambda c, s: (c, s ^ k)) for k in (1, 2, 3)]
     co, yo = [send(x, lambda c, s: (c ^ k, s)) for k in (1, 2)]
-    xv, lines, columns, z2, z3, z1, yo, co = lax.optimization_barrier((xv, lines, columns, z2, z3, z1, yo, co))
+    xv, lines, columns, near, z2, z3, z1, yo, co = lax.optimization_barrier((xv, lines, columns, near, z2, z3, z1, yo, co))
     cz = send(jnp.concatenate([z1, z2, z3]), lambda c, s: (c ^ 1, s))
     cyo = send(yo, lambda c, s: (c ^ 1, s))
-    space = scratch(rows, width) + [pltpu.VMEM((4 * rows, width), x.dtype)]
-    sums = jax.ShapeDtypeStruct(sums_shape(rows), f32)
-    pair = jax.ShapeDtypeStruct(sums_shape(rows, 2), f32)
     across = pl.pallas_call(
         functools.partial(across_kernel, scale=scale),
-        out_shape=pair,
+        out_shape=sums(2),
         in_specs=[VMEM] * 7,
         out_specs=VMEM,
-        scratch_shapes=space,
+        scratch_shapes=space(4),
         compiler_params=PARAMS,
     )(yo, z1, z2, z3, cz, lines, columns)
     there = send(across, lambda c, s: (c ^ 2, s))
-    here, own = pl.pallas_call(
+    here = pl.pallas_call(
         functools.partial(here_kernel, scale=scale),
-        out_shape=[pair, sums],
+        out_shape=sums(3),
         in_specs=[VMEM] * 10,
-        out_specs=[VMEM] * 2,
-        scratch_shapes=space,
+        out_specs=VMEM,
+        scratch_shapes=space(7),
         compiler_params=PARAMS,
     )(xv, co, yo, cyo, z1, z2, z3, cz, lines, columns)
     stacks = pl.pallas_call(
         join_kernel,
-        out_shape=jax.ShapeDtypeStruct((3, rows, 2 * LAGS), f32),
+        out_shape=jax.ShapeDtypeStruct((3, rows, 2 * LAGS), jnp.float32),
         in_specs=[VMEM] * 3,
         out_specs=VMEM,
         compiler_params=PARAMS,
-    )(own, here, there)
+    )(near, here, there)
     return jnp.transpose(stacks, (1, 0, 2))
 
 

time: 20.7 us -> 20.5 us (level)
  waiting for transfers between devices: 2.71 us -> 1.01 us
  Pallas kernels: 8.49 us -> 10 us
    ppermute x8, waiting for transfers between devices: 2.71 us -> 1.01 us  [send(): return lax.ppermute(x, ('chan', 'sect'), pairs)]
    pallas_call x3, Pallas kernels: 7.6 us -> 9.16 us  [the longest x1 3.51 us: stacks_by_flips(): pl.pallas_call(functools.partial(here_kernel, scale=scale), out_shape=sum...]
  transfers between devices with their start and end apart: 8 -> 8, of which waited for: 3 -> 1; matrix products, arithmetic and copies ran while one was open for 0% -> 0% of each run, Pallas kernels for 37% -> 45%
where the time goes in v5:
time: 20.5 us; the launch traced here: 20.4 us
  Pallas kernels  10 us (49%)
  starting transfers between devices  9.21 us (45%)
  waiting for transfers between devices  1.01 us (5%)
    ppermute x8, starting transfers between devices, send(): return lax.ppermute(x, ('chan', 'sect'), pairs)  9.21 us
    pallas_call x1, Pallas kernels, stacks_by_flips(): pl.pallas_call(functools.partial(here_kernel, scale=scale), out_shape=sum...  3.51 us
    pallas_call x1, Pallas kernels, stacks_by_flips(): pl.pallas_call(functools.partial(first_kernel, scale=scale), out_shape=[j...  3.39 us
    pallas_call x1, Pallas kernels, stacks_by_flips(): pl.pallas_call(functools.partial(across_kernel, scale=scale), out_shape=s...  2.25 us
    ppermute x8, waiting for transfers between devices, send(): return lax.ppermute(x, ('chan', 'sect'), pairs)  1.01 us
    pallas_call x1, Pallas kernels, stacks_by_flips(): pl.pallas_call(join_kernel, out_shape=jax.ShapeDtypeStruct((3, rows, 2 *...  0.89 us
  transfers between devices with their start and end apart: 8, of which 1 were waited for; matrix products, arithmetic and copies ran while one was open for 0% of the time, Pallas kernels for 45%

profile of v5, /device:TPU:0, one launch (start us, length us, event | category | flops | bytes accessed | tf_op | source)
XLA Modules:
  0.0 20.4 jit_solution(6625992765505940964)
XLA Ops:
  0.0 0.0 copy-start
  0.0 4.0 %collective-permute-start = (bf16[64,512]{1,0:T(8,128)(2,1)}, bf16[64,512]{1,0:T(8,128)(2,1)S(1)}, u32[]{:S(2)}, u32[]{:S(2)}) collective-permute-start(bf16[64,512]{1,0:T(8,128)(2,1)} %bitcast.6), channel_id=1, source_target_pairs={{0,2},{1,3},{2,0},{3,1},{4,6},{5,7},{6,4},{7,5},{8,10},{9,11},{10,... | collective-permute-start | bytes 196616 | tf_op jit(solution)/shard_map/ppermute | solution.py:260
  4.0 1.3 %collective-permute-start.1 = (bf16[64,512]{1,0:T(8,128)(2,1)}, bf16[64,512]{1,0:T(8,128)(2,1)S(1)}, u32[]{:S(2)}, u32[]{:S(2)}) collective-permute-start(bf16[64,512]{1,0:T(8,128)(2,1)} %bitcast.7), channel_id=1, source_target_pairs={{0,3},{1,2},{2,1},{3,0},{4,7},{5,6},{6,5},{7,4},{8,11},{9,10},{10,... | collective-permute-start | bytes 196616 | tf_op jit(solution)/shard_map/ppermute | solution.py:260
  5.4 0.2 %collective-permute-start.2 = (bf16[64,512]{1,0:T(8,128)(2,1)}, bf16[64,512]{1,0:T(8,128)(2,1)S(1)}, u32[]{:S(2)}, u32[]{:S(2)}) collective-permute-start(bf16[64,512]{1,0:T(8,128)(2,1)} %bitcast.8), channel_id=1, source_target_pairs={{0,1},{1,0},{2,3},{3,2},{4,5},{5,4},{6,7},{7,6},{8,9},{9,8},{10,11... | collective-permute-start | bytes 196616 | tf_op jit(solution)/shard_map/ppermute | solution.py:260
  5.6 1.5 %collective-permute-start.3 = (bf16[64,512]{1,0:T(8,128)(2,1)}, bf16[64,512]{1,0:T(8,128)(2,1)S(1)}, u32[]{:S(2)}, u32[]{:S(2)}) collective-permute-start(bf16[64,512]{1,0:T(8,128)(2,1)} %bitcast.9), channel_id=1, source_target_pairs={{0,8},{1,9},{2,10},{3,11},{4,12},{5,13},{6,14},{7,15},{8,0},{9,1},... | collective-permute-start | bytes 196616 | tf_op jit(solution)/shard_map/ppermute | solution.py:260
  7.1 0.0 collective-permute-start.4
  7.1 0.0 copy-done
  7.1 3.4 %shard_map.37 = (bf16[64,512]{1,0:T(8,128)(2,1)S(1)}, f32[8,128]{1,0:T(8,128)S(1)}, f32[448,128]{1,0:T(8,128)S(1)}, f32[64,128]{1,0:T(8,128)S(1)}) custom-call(s32[2,4]{1,0:T(2,128)S(1)} %bitcast.5, bf16[64,512]{1,0:T(8,128)(2,1)} %bitcast.11, s32[4,256]{1,0:T(4,128)} %pos_ref.1), custom_call_target="tpu_custom_call" | custom-call | tf_op jit(solution)/shard_map/pallas_call | solution.py:268
  10.5 0.0 collective-permute-done.z2_ref
  10.6 0.0 collective-permute-done.1.z3_ref
  10.6 0.0 collective-permute-done.2.z1_ref
  10.6 0.0 collective-permute-done.3.yo_ref
  10.6 0.0 collective-permute-done.4.co_ref
  10.6 0.6 %collective-permute-start.6 = (bf16[192,512]{1,0:T(8,128)(2,1)S(1)}, bf16[192,512]{1,0:T(8,128)(2,1)S(1)}, u32[]{:S(2)}, u32[]{:S(2)}) collective-permute-start(bf16[192,512]{1,0:T(8,128)(2,1)S(1)} %pad_maximum_fusion), channel_id=1, source_target_pairs={{0,4},{1,5},{2,6},{3,7},{4,0},{5,1},{6,2},{7,3},{8,12},{9,13},{10,... | collective-permute-start | bytes 589832 | tf_op jit(solution)/shard_map/ppermute | solution.py:260
  11.2 0.1 collective-permute-start.5
  11.3 1.0 %collective-permute-done.6.cz_ref = bf16[192,512]{1,0:T(8,128)(2,1)S(1)} collective-permute-done((bf16[192,512]{1,0:T(8,128)(2,1)S(1)}, bf16[192,512]{1,0:T(8,128)(2,1)S(1)}, u32[]{:S(2)}, u32[]{:S(2)}) %collective-permute-start.6) | collective-permute-done | bytes 196640 | tf_op jit(solution)/shard_map/ppermute | solution.py:260
  12.3 2.3 %shard_map.39 = f32[2,64,128]{2,1,0:T(8,128)S(1)} custom-call(bf16[64,512]{1,0:T(8,128)(2,1)S(1)} %collective-permute-done.3.yo_ref, bf16[64,512]{1,0:T(8,128)(2,1)S(1)} %collective-permute-done.2.z1_ref, bf16[64,512]{1,0:T(8,128)(2,1)S(1)} %collective-permute-done.z2_ref, bf16[64,512]{1,0:T(8,128)(2,1)S(1)} %collective-permute-done.1.z3_ref, ...), custom_call_target="tpu_custom_call" | custom-call | tf_op jit(solution)/shard_map/pallas_call | solution.py:287
  14.5 1.4 %collective-permute-start.7 = (f32[2,64,128]{2,1,0:T(8,128)S(1)}, f32[2,64,128]{2,1,0:T(8,128)S(1)}, u32[]{:S(2)}, u32[]{:S(2)}) collective-permute-start(f32[2,64,128]{2,1,0:T(8,128)S(1)} %shard_map.39), channel_id=1, source_target_pairs={{0,8},{1,9},{2,10},{3,11},{4,12},{5,13},{6,14},{7,15},{8,0},{9,1},... | collective-permute-start | bytes 196616 | tf_op jit(solution)/shard_map/ppermute | solution.py:260
  15.9 0.0 collective-permute-done.5.cyo_ref
  15.9 3.5 %shard_map.38.here_ref = f32[3,64,128]{2,1,0:T(8,128)S(1)} custom-call(bf16[64,512]{1,0:T(8,128)(2,1)S(1)} %get-tuple-element.23.x_ref, bf16[64,512]{1,0:T(8,128)(2,1)S(1)} %collective-permute-done.4.co_ref, bf16[64,512]{1,0:T(8,128)(2,1)S(1)} %collective-permute-done.3.yo_ref, bf16[64,512]{1,0:T(8,128)(2,1)S(1)} %collective-permute-done.5.cyo_ref, ...), custom_call_target="tpu_custom_call" | custom-call | tf_op jit(solution)/shard_map/pallas_call | solution.py:296
  19.5 0.0 collective-permute-done.7.there_ref
  19.5 0.9 %shard_map.40 = f32[3,64,128]{2,1,0:T(8,128)} custom-call(f32[64,128]{1,0:T(8,128)S(1)} %get-tuple-element.22.own_ref, f32[3,64,128]{2,1,0:T(8,128)S(1)} %shard_map.38.here_ref, f32[2,64,128]{2,1,0:T(8,128)S(1)} %collective-permute-done.7.there_ref), custom_call_target="tpu_custom_call" | custom-call | tf_op jit(solution)/shard_map/pallas_call | solution.py:304
  (1 shorter events, 0.0 us)
Async XLA Ops:
  0.0 7.1 %copy-start = (s32[4,2]{0,1:T(2,128)S(1)}, s32[4,2]{0,1:T(2,128)}, u32[]{:S(2)}) copy-start(s32[4,2]{0,1:T(2,128)} %param.5) | copy-start | bytes 100
  0.0 10.5 %collective-permute-start = (bf16[64,512]{1,0:T(8,128)(2,1)}, bf16[64,512]{1,0:T(8,128)(2,1)S(1)}, u32[]{:S(2)}, u32[]{:S(2)}) collective-permute-start(bf16[64,512]{1,0:T(8,128)(2,1)} %bitcast.6), channel_id=1, source_target_pairs={{0,2},{1,3},{2,0},{3,1},{4,6},{5,7},{6,4},{7,5},{8,10},{9,11},{10,... | collective-permute-start | bytes 196616 | tf_op jit(solution)/shard_map/ppermute | solution.py:260
  4.0 6.5 %collective-permute-start.1 = (bf16[64,512]{1,0:T(8,128)(2,1)}, bf16[64,512]{1,0:T(8,128)(2,1)S(1)}, u32[]{:S(2)}, u32[]{:S(2)}) collective-permute-start(bf16[64,512]{1,0:T(8,128)(2,1)} %bitcast.7), channel_id=1, source_target_pairs={{0,3},{1,2},{2,1},{3,0},{4,7},{5,6},{6,5},{7,4},{8,11},{9,10},{10,... | collective-permute-start | bytes 196616 | tf_op jit(solution)/shard_map/ppermute | solution.py:260
  5.4 5.2 %collective-permute-start.2 = (bf16[64,512]{1,0:T(8,128)(2,1)}, bf16[64,512]{1,0:T(8,128)(2,1)S(1)}, u32[]{:S(2)}, u32[]{:S(2)}) collective-permute-start(bf16[64,512]{1,0:T(8,128)(2,1)} %bitcast.8), channel_id=1, source_target_pairs={{0,1},{1,0},{2,3},{3,2},{4,5},{5,4},{6,7},{7,6},{8,9},{9,8},{10,11... | collective-permute-start | bytes 196616 | tf_op jit(solution)/shard_map/ppermute | solution.py:260
  5.6 5.0 %collective-permute-start.3 = (bf16[64,512]{1,0:T(8,128)(2,1)}, bf16[64,512]{1,0:T(8,128)(2,1)S(1)}, u32[]{:S(2)}, u32[]{:S(2)}) collective-permute-start(bf16[64,512]{1,0:T(8,128)(2,1)} %bitcast.9), channel_id=1, source_target_pairs={{0,8},{1,9},{2,10},{3,11},{4,12},{5,13},{6,14},{7,15},{8,0},{9,1},... | collective-permute-start | bytes 196616 | tf_op jit(solution)/shard_map/ppermute | solution.py:260
  7.1 3.5 %collective-permute-start.4 = (bf16[64,512]{1,0:T(8,128)(2,1)}, bf16[64,512]{1,0:T(8,128)(2,1)S(1)}, u32[]{:S(2)}, u32[]{:S(2)}) collective-permute-start(bf16[64,512]{1,0:T(8,128)(2,1)} %bitcast.10), channel_id=1, source_target_pairs={{0,4},{1,5},{2,6},{3,7},{4,0},{5,1},{6,2},{7,3},{8,12},{9,13},{10,... | collective-permute-start | bytes 196616 | tf_op jit(solution)/shard_map/ppermute | solution.py:260
  10.6 1.6 %collective-permute-start.6 = (bf16[192,512]{1,0:T(8,128)(2,1)S(1)}, bf16[192,512]{1,0:T(8,128)(2,1)S(1)}, u32[]{:S(2)}, u32[]{:S(2)}) collective-permute-start(bf16[192,512]{1,0:T(8,128)(2,1)S(1)} %pad_maximum_fusion), channel_id=1, source_target_pairs={{0,4},{1,5},{2,6},{3,7},{4,0},{5,1},{6,2},{7,3},{8,12},{9,13},{10,... | collective-permute-start | bytes 589832 | tf_op jit(solution)/shard_map/ppermute | solution.py:260
  11.2 4.8 %collective-permute-start.5 = (bf16[64,512]{1,0:T(8,128)(2,1)S(1)}, bf16[64,512]{1,0:T(8,128)(2,1)S(1)}, u32[]{:S(2)}, u32[]{:S(2)}) collective-permute-start(bf16[64,512]{1,0:T(8,128)(2,1)S(1)} %collective-permute-done.3.yo_ref), channel_id=1, source_target_pairs={{0,4},{1,5},{2,6},{3,7},{4,0},{5,1},{6,2},{7,3},{8,12},{9,13},{10,... | collective-permute-start | bytes 196616 | tf_op jit(solution)/shard_map/ppermute | solution.py:260
  14.5 4.9 %collective-permute-start.7 = (f32[2,64,128]{2,1,0:T(8,128)S(1)}, f32[2,64,128]{2,1,0:T(8,128)S(1)}, u32[]{:S(2)}, u32[]{:S(2)}) collective-permute-start(f32[2,64,128]{2,1,0:T(8,128)S(1)} %shard_map.39), channel_id=1, source_target_pairs={{0,8},{1,9},{2,10},{3,11},{4,12},{5,13},{6,14},{7,15},{8,0},{9,1},... | collective-permute-start | bytes 196616 | tf_op jit(solution)/shard_map/ppermute | solution.py:260

commit v6 on v5

--- a/solution.py
+++ b/solution.py
@@ -224,7 +224,7 @@
 
 
 def across_kernel(
-    yo_ref, z1_ref, z2_ref, z3_ref, cz_ref, rows_ref, cols_ref, o_ref, t_ref, c_ref, w_ref, xs_ref, *, scale
+    yo_ref, z1_ref, z2_ref, z3_ref, cz_ref, rows_ref, cols_ref, o_ref, xs_ref, t_ref, c_ref, w_ref, *, scale
 ):
     rows = yo_ref.shape[0]
     build_windows(yo_ref[...], t_ref)
@@ -233,11 +233,11 @@
 
 
 def here_kernel(
-    x_ref, co_ref, yo_ref, cyo_ref, z1_ref, z2_ref, z3_ref, cz_ref, rows_ref, cols_ref, o_ref, t_ref, c_ref, w_ref, xs_ref, *, scale
+    x_ref, co_ref, yo_ref, cyo_ref, picked_ref, rows_ref, cols_ref, o_ref, t_ref, c_ref, w_ref, xs_ref, *, scale
 ):
     rows = x_ref.shape[0]
     build_windows(x_ref[...], t_ref)
-    gather_pairs((z1_ref, z2_ref, z3_ref), cz_ref, rows_ref, xs_ref, rows)
+    xs_ref[0 : 4 * rows, :] = picked_ref[...]
     for k, ref in enumerate((co_ref, yo_ref, cyo_ref)):
         xs_ref[(4 + k) * rows : (5 + k) * rows, :] = ref[...]
     target_sums(xs_ref, t_ref, c_ref, w_ref, rows_ref[0:1, :], cols_ref, o_ref, scale)
@@ -284,23 +284,23 @@
     xv, lines, columns, near, z2, z3, z1, yo, co = lax.optimization_barrier((xv, lines, columns, near, z2, z3, z1, yo, co))
     cz = send(jnp.concatenate([z1, z2, z3]), lambda c, s: (c ^ 1, s))
     cyo = send(yo, lambda c, s: (c ^ 1, s))
-    across = pl.pallas_call(
+    across, picked = pl.pallas_call(
         functools.partial(across_kernel, scale=scale),
-        out_shape=sums(2),
+        out_shape=[sums(2), jax.ShapeDtypeStruct((4 * rows, width), x.dtype)],
         in_specs=[VMEM] * 7,
-        out_specs=VMEM,
-        scratch_shapes=space(4),
+        out_specs=[VMEM] * 2,
+        scratch_shapes=scratch(rows, width, 4 * rows),
         compiler_params=PARAMS,
     )(yo, z1, z2, z3, cz, lines, columns)
     there = send(across, lambda c, s: (c ^ 2, s))
     here = pl.pallas_call(
         functools.partial(here_kernel, scale=scale),
         out_shape=sums(3),
-        in_specs=[VMEM] * 10,
+        in_specs=[VMEM] * 7,
         out_specs=VMEM,
         scratch_shapes=space(7),
         compiler_params=PARAMS,
-    )(xv, co, yo, cyo, z1, z2, z3, cz, lines, columns)
+    )(xv, co, yo, cyo, picked, lines, columns)
     stacks = pl.pallas_call(
         join_kernel,
         out_shape=jax.ShapeDtypeStruct((3, rows, 2 * LAGS), jnp.float32),

time: 20.5 us -> 20.6 us (level)
  no operation moved by 1% of the time
where the time goes in v6:
time: 20.6 us; the launch traced here: 20.4 us
  Pallas kernels  10.1 us (49%)
  starting transfers between devices  9.21 us (45%)
  waiting for transfers between devices  1.01 us (5%)
    ppermute x8, starting transfers between devices, send(): return lax.ppermute(x, ('chan', 'sect'), pairs)  9.21 us
    pallas_call x1, Pallas kernels, stacks_by_flips(): pl.pallas_call(functools.partial(here_kernel, scale=scale), out_shape=sum...  3.53 us
    pallas_call x1, Pallas kernels, stacks_by_flips(): pl.pallas_call(functools.partial(first_kernel, scale=scale), out_shape=[j...  3.39 us
    pallas_call x1, Pallas kernels, stacks_by_flips(): pl.pallas_call(functools.partial(across_kernel, scale=scale), out_shape=[...  2.27 us
    ppermute x8, waiting for transfers between devices, send(): return lax.ppermute(x, ('chan', 'sect'), pairs)  1.01 us
    pallas_call x1, Pallas kernels, stacks_by_flips(): pl.pallas_call(join_kernel, out_shape=jax.ShapeDtypeStruct((3, rows, 2 *...  0.88 us
  transfers between devices with their start and end apart: 8, of which 1 were waited for; matrix products, arithmetic and copies ran while one was open for 0% of the time, Pallas kernels for 45%

profile of v6, /device:TPU:0, one launch (start us, length us, event | category | flops | bytes accessed | tf_op | source)
XLA Modules:
  0.0 20.4 jit_solution(3559567471626370100)
XLA Ops:
  0.0 0.0 copy-start
  0.0 4.0 %collective-permute-start = (bf16[64,512]{1,0:T(8,128)(2,1)}, bf16[64,512]{1,0:T(8,128)(2,1)S(1)}, u32[]{:S(2)}, u32[]{:S(2)}) collective-permute-start(bf16[64,512]{1,0:T(8,128)(2,1)} %bitcast.6), channel_id=1, source_target_pairs={{0,2},{1,3},{2,0},{3,1},{4,6},{5,7},{6,4},{7,5},{8,10},{9,11},{10,... | collective-permute-start | bytes 196616 | tf_op jit(solution)/shard_map/ppermute | solution.py:260
  4.0 1.3 %collective-permute-start.1 = (bf16[64,512]{1,0:T(8,128)(2,1)}, bf16[64,512]{1,0:T(8,128)(2,1)S(1)}, u32[]{:S(2)}, u32[]{:S(2)}) collective-permute-start(bf16[64,512]{1,0:T(8,128)(2,1)} %bitcast.7), channel_id=1, source_target_pairs={{0,3},{1,2},{2,1},{3,0},{4,7},{5,6},{6,5},{7,4},{8,11},{9,10},{10,... | collective-permute-start | bytes 196616 | tf_op jit(solution)/shard_map/ppermute | solution.py:260
  5.4 0.2 %collective-permute-start.2 = (bf16[64,512]{1,0:T(8,128)(2,1)}, bf16[64,512]{1,0:T(8,128)(2,1)S(1)}, u32[]{:S(2)}, u32[]{:S(2)}) collective-permute-start(bf16[64,512]{1,0:T(8,128)(2,1)} %bitcast.8), channel_id=1, source_target_pairs={{0,1},{1,0},{2,3},{3,2},{4,5},{5,4},{6,7},{7,6},{8,9},{9,8},{10,11... | collective-permute-start | bytes 196616 | tf_op jit(solution)/shard_map/ppermute | solution.py:260
  5.6 1.5 %collective-permute-start.3 = (bf16[64,512]{1,0:T(8,128)(2,1)}, bf16[64,512]{1,0:T(8,128)(2,1)S(1)}, u32[]{:S(2)}, u32[]{:S(2)}) collective-permute-start(bf16[64,512]{1,0:T(8,128)(2,1)} %bitcast.9), channel_id=1, source_target_pairs={{0,8},{1,9},{2,10},{3,11},{4,12},{5,13},{6,14},{7,15},{8,0},{9,1},... | collective-permute-start | bytes 196616 | tf_op jit(solution)/shard_map/ppermute | solution.py:260
  7.1 0.0 collective-permute-start.4
  7.1 0.0 copy-done
  7.1 3.4 %shard_map.37 = (bf16[64,512]{1,0:T(8,128)(2,1)S(1)}, f32[8,128]{1,0:T(8,128)S(1)}, f32[448,128]{1,0:T(8,128)S(1)}, f32[64,128]{1,0:T(8,128)S(1)}) custom-call(s32[2,4]{1,0:T(2,128)S(1)} %bitcast.5, bf16[64,512]{1,0:T(8,128)(2,1)} %bitcast.11, s32[4,256]{1,0:T(4,128)} %pos_ref.1), custom_call_target="tpu_custom_call" | custom-call | tf_op jit(solution)/shard_map/pallas_call | solution.py:268
  10.5 0.0 collective-permute-done.z2_ref
  10.6 0.0 collective-permute-done.1.z3_ref
  10.6 0.0 collective-permute-done.2.z1_ref
  10.6 0.0 collective-permute-done.3.yo_ref
  10.6 0.0 collective-permute-done.4.co_ref
  10.6 0.6 %collective-permute-start.6 = (bf16[192,512]{1,0:T(8,128)(2,1)S(1)}, bf16[192,512]{1,0:T(8,128)(2,1)S(1)}, u32[]{:S(2)}, u32[]{:S(2)}) collective-permute-start(bf16[192,512]{1,0:T(8,128)(2,1)S(1)} %pad_maximum_fusion), channel_id=1, source_target_pairs={{0,4},{1,5},{2,6},{3,7},{4,0},{5,1},{6,2},{7,3},{8,12},{9,13},{10,... | collective-permute-start | bytes 589832 | tf_op jit(solution)/shard_map/ppermute | solution.py:260
  11.2 0.1 collective-permute-start.5
  11.3 1.0 %collective-permute-done.6.cz_ref = bf16[192,512]{1,0:T(8,128)(2,1)S(1)} collective-permute-done((bf16[192,512]{1,0:T(8,128)(2,1)S(1)}, bf16[192,512]{1,0:T(8,128)(2,1)S(1)}, u32[]{:S(2)}, u32[]{:S(2)}) %collective-permute-start.6) | collective-permute-done | bytes 196640 | tf_op jit(solution)/shard_map/ppermute | solution.py:260
  12.3 2.3 %shard_map.38 = (f32[2,64,128]{2,1,0:T(8,128)S(1)}, bf16[256,512]{1,0:T(8,128)(2,1)S(1)}) custom-call(bf16[64,512]{1,0:T(8,128)(2,1)S(1)} %collective-permute-done.3.yo_ref, bf16[64,512]{1,0:T(8,128)(2,1)S(1)} %collective-permute-done.2.z1_ref, bf16[64,512]{1,0:T(8,128)(2,1)S(1)} %collective-permute-done.z2_ref, ...), custom_call_target="tpu_custom_call" | custom-call | tf_op jit(solution)/shard_map/pallas_call | solution.py:287
  14.5 1.4 %collective-permute-start.7 = (f32[2,64,128]{2,1,0:T(8,128)S(1)}, f32[2,64,128]{2,1,0:T(8,128)S(1)}, u32[]{:S(2)}, u32[]{:S(2)}) collective-permute-start(f32[2,64,128]{2,1,0:T(8,128)S(1)} %get-tuple-element.34), channel_id=1, source_target_pairs={{0,8},{1,9},{2,10},{3,11},{4,12},{5,13},{6,14},{7,15},{8,0},{9,1},... | collective-permute-start | bytes 196616 | tf_op jit(solution)/shard_map/ppermute | solution.py:260
  16.0 0.0 collective-permute-done.5.cyo_ref
  16.0 3.5 %shard_map.39.here_ref = f32[3,64,128]{2,1,0:T(8,128)S(1)} custom-call(bf16[64,512]{1,0:T(8,128)(2,1)S(1)} %get-tuple-element.25.x_ref, bf16[64,512]{1,0:T(8,128)(2,1)S(1)} %collective-permute-done.4.co_ref, bf16[64,512]{1,0:T(8,128)(2,1)S(1)} %collective-permute-done.3.yo_ref, bf16[64,512]{1,0:T(8,128)(2,1)S(1)} %collective-permute-done.5.cyo_ref, ...), custom_call_target="tpu_custom_call" | custom-call | tf_op jit(solution)/shard_map/pallas_call | solution.py:296
  19.5 0.0 collective-permute-done.7.there_ref
  19.5 0.9 %shard_map.40 = f32[3,64,128]{2,1,0:T(8,128)} custom-call(f32[64,128]{1,0:T(8,128)S(1)} %get-tuple-element.24.own_ref, f32[3,64,128]{2,1,0:T(8,128)S(1)} %shard_map.39.here_ref, f32[2,64,128]{2,1,0:T(8,128)S(1)} %collective-permute-done.7.there_ref), custom_call_target="tpu_custom_call" | custom-call | tf_op jit(solution)/shard_map/pallas_call | solution.py:304
  (1 shorter events, 0.0 us)
Async XLA Ops:
  0.0 7.1 %copy-start = (s32[4,2]{0,1:T(2,128)S(1)}, s32[4,2]{0,1:T(2,128)}, u32[]{:S(2)}) copy-start(s32[4,2]{0,1:T(2,128)} %param.5) | copy-start | bytes 100
  0.0 10.5 %collective-permute-start = (bf16[64,512]{1,0:T(8,128)(2,1)}, bf16[64,512]{1,0:T(8,128)(2,1)S(1)}, u32[]{:S(2)}, u32[]{:S(2)}) collective-permute-start(bf16[64,512]{1,0:T(8,128)(2,1)} %bitcast.6), channel_id=1, source_target_pairs={{0,2},{1,3},{2,0},{3,1},{4,6},{5,7},{6,4},{7,5},{8,10},{9,11},{10,... | collective-permute-start | bytes 196616 | tf_op jit(solution)/shard_map/ppermute | solution.py:260
  4.0 6.5 %collective-permute-start.1 = (bf16[64,512]{1,0:T(8,128)(2,1)}, bf16[64,512]{1,0:T(8,128)(2,1)S(1)}, u32[]{:S(2)}, u32[]{:S(2)}) collective-permute-start(bf16[64,512]{1,0:T(8,128)(2,1)} %bitcast.7), channel_id=1, source_target_pairs={{0,3},{1,2},{2,1},{3,0},{4,7},{5,6},{6,5},{7,4},{8,11},{9,10},{10,... | collective-permute-start | bytes 196616 | tf_op jit(solution)/shard_map/ppermute | solution.py:260
  5.4 5.2 %collective-permute-start.2 = (bf16[64,512]{1,0:T(8,128)(2,1)}, bf16[64,512]{1,0:T(8,128)(2,1)S(1)}, u32[]{:S(2)}, u32[]{:S(2)}) collective-permute-start(bf16[64,512]{1,0:T(8,128)(2,1)} %bitcast.8), channel_id=1, source_target_pairs={{0,1},{1,0},{2,3},{3,2},{4,5},{5,4},{6,7},{7,6},{8,9},{9,8},{10,11... | collective-permute-start | bytes 196616 | tf_op jit(solution)/shard_map/ppermute | solution.py:260
  5.6 5.0 %collective-permute-start.3 = (bf16[64,512]{1,0:T(8,128)(2,1)}, bf16[64,512]{1,0:T(8,128)(2,1)S(1)}, u32[]{:S(2)}, u32[]{:S(2)}) collective-permute-start(bf16[64,512]{1,0:T(8,128)(2,1)} %bitcast.9), channel_id=1, source_target_pairs={{0,8},{1,9},{2,10},{3,11},{4,12},{5,13},{6,14},{7,15},{8,0},{9,1},... | collective-permute-start | bytes 196616 | tf_op jit(solution)/shard_map/ppermute | solution.py:260
  7.1 3.5 %collective-permute-start.4 = (bf16[64,512]{1,0:T(8,128)(2,1)}, bf16[64,512]{1,0:T(8,128)(2,1)S(1)}, u32[]{:S(2)}, u32[]{:S(2)}) collective-permute-start(bf16[64,512]{1,0:T(8,128)(2,1)} %bitcast.10), channel_id=1, source_target_pairs={{0,4},{1,5},{2,6},{3,7},{4,0},{5,1},{6,2},{7,3},{8,12},{9,13},{10,... | collective-permute-start | bytes 196616 | tf_op jit(solution)/shard_map/ppermute | solution.py:260
  10.6 1.6 %collective-permute-start.6 = (bf16[192,512]{1,0:T(8,128)(2,1)S(1)}, bf16[192,512]{1,0:T(8,128)(2,1)S(1)}, u32[]{:S(2)}, u32[]{:S(2)}) collective-permute-start(bf16[192,512]{1,0:T(8,128)(2,1)S(1)} %pad_maximum_fusion), channel_id=1, source_target_pairs={{0,4},{1,5},{2,6},{3,7},{4,0},{5,1},{6,2},{7,3},{8,12},{9,13},{10,... | collective-permute-start | bytes 589832 | tf_op jit(solution)/shard_map/ppermute | solution.py:260
  11.2 4.8 %collective-permute-start.5 = (bf16[64,512]{1,0:T(8,128)(2,1)S(1)}, bf16[64,512]{1,0:T(8,128)(2,1)S(1)}, u32[]{:S(2)}, u32[]{:S(2)}) collective-permute-start(bf16[64,512]{1,0:T(8,128)(2,1)S(1)} %collective-permute-done.3.yo_ref), channel_id=1, source_target_pairs={{0,4},{1,5},{2,6},{3,7},{4,0},{5,1},{6,2},{7,3},{8,12},{9,13},{10,... | collective-permute-start | bytes 196616 | tf_op jit(solution)/shard_map/ppermute | solution.py:260
  14.5 5.0 %collective-permute-start.7 = (f32[2,64,128]{2,1,0:T(8,128)S(1)}, f32[2,64,128]{2,1,0:T(8,128)S(1)}, u32[]{:S(2)}, u32[]{:S(2)}) collective-permute-start(f32[2,64,128]{2,1,0:T(8,128)S(1)} %get-tuple-element.34), channel_id=1, source_target_pairs={{0,8},{1,9},{2,10},{3,11},{4,12},{5,13},{6,14},{7,15},{8,0},{9,1},... | collective-permute-start | bytes 196616 | tf_op jit(solution)/shard_map/ppermute | solution.py:260
